TPU v7x, 32 devices: a whole 2x2x4 slice. The times are simulated.
32 devices in a mesh: dom: 16 (over z, y, x), chan: 2 (over core).
Axes of the slice: x: 2, y: 2, z: 4, core: 2. Of those that a mesh axis runs over, the one named last changes fastest.
Arguments:
- features: bfloat16 [16384, 512], P('dom', 'chan'), may hold values from -6 to 6
- w_self: bfloat16 [512, 512], P('chan'), may hold values from -0.25 to 0.25
- w_neigh: bfloat16 [512, 512], P('chan'), may hold values from -1.5 to 1.5
- degrees: int32 [16384], P('dom'), may hold values from 16 to 48
- local_src: int32 [128], P('dom'), may hold values from 0 to 7
- local_dst: int32 [128], P('dom'), may hold values from 0 to 7
- local_tiles: bfloat16 [128, 128, 128], P('dom'), may hold values from 0 to 1, as said below
- remote_src: int32 [256], P('dom'), may hold values from 0 to 7
- remote_part: int32 [256, 1], P('dom'), may hold values from 0 to 15; in each aligned block of 16 rows (0 to 15, 16 to 31, ...) at most 2 rows name the same one
- remote_dst: int32 [256], P('dom'), may hold values from 0 to 7
- remote_tiles: bfloat16 [256, 128, 128], P('dom'), may hold values from 0 to 1, as said below
- cotangent: bfloat16 [16384, 512], P('dom', 'chan'), may hold values from -6 to 6
Outputs:
- output: bfloat16 [16384, 512], P('dom', 'chan')
- grad_self: float32 [512, 512], P('chan')
- grad_neigh: float32 [512, 512], P('chan')
- grad_features: bfloat16 [16384, 512], P('dom', 'chan')
Inputs may be any that keep to these rules, and one draw needn't show every extreme that they name: `remote_part`: among the 16 remote tiles of one partition each partition is named at most 2 times, a bound that some block reaches. `local_tiles`: every entry is 0 or 1. `remote_tiles`: every entry is 0 or 1.
All inputs are finite; a program needn't handle non-finite values.
Results may differ from a plain program's by a relative error of at most 0.015.
Values may be sent and summed in bfloat16 or wider, within the bound.
No kernel may reach another device: no remote copies, remote signals or barrier semaphores. Data moves between devices by JAX's collectives and lax.ppermute only.
A program may use at most 64 MiB of HBM per device.

v0:
```python
import math

import jax
import jax.numpy as jnp
from jax import lax
from jax.experimental import pallas as pl
from jax.experimental.pallas import tpu as pltpu
from jax.sharding import PartitionSpec as P


TILE = 128
CAP = 2
TAG_ROWS = 8
PAIR = CAP * TILE

F32 = jnp.float32
BF16 = jnp.bfloat16
I32 = jnp.int32
VMEM = pl.BlockSpec(memory_space=pltpu.VMEM)
SMEM = pl.BlockSpec(memory_space=pltpu.SMEM)
HBM = pl.BlockSpec(memory_space=pltpu.HBM)


def shape(dims, dtype):
    return jax.ShapeDtypeStruct(dims, dtype)


def call(kernel, outs, ins, scratch=(), flops=1 << 20, limit=16 * 1024 * 1024, nbytes=1 << 20):
    return pl.pallas_call(
        kernel,
        out_shape=tuple(out for _, out in outs),
        in_specs=[spec for spec, _ in ins],
        out_specs=tuple(spec for spec, _ in outs),
        scratch_shapes=list(scratch),
        compiler_params=pltpu.CompilerParams(vmem_limit_bytes=limit),
        cost_estimate=pl.CostEstimate(flops=flops, bytes_accessed=nbytes, transcendentals=0),
    )(*[array for _, array in ins])


def vmem(arrays):
    return [(VMEM, array) for array in arrays]


def smem(arrays):
    return [(SMEM, array) for array in arrays]


def dot_tn(a, b):
    return lax.dot_general(a, b, (((0,), (0,)), ((), ())), preferred_element_type=F32)


def dot_nn(a, b):
    return lax.dot_general(a, b, (((1,), (0,)), ((), ())), preferred_element_type=F32)


def dot_nt(a, b):
    return lax.dot_general(a, b, (((1,), (1,)), ((), ())), preferred_element_type=F32)


def block_at(number):
    return slice(number * TILE, (number + 1) * TILE)


def fill_slots(part, count, slots, tiles):
    for place in range(count.shape[0]):
        count[place] = 0
    for place in range(slots.shape[0]):
        slots[place] = -1
    for number in range(tiles):
        target = part[number]
        place = count[target]
        count[target] = place + 1
        slots[target * CAP + place] = number


def degree_columns(degrees):
    return jnp.transpose(degrees[...].astype(F32))


def place_tiles(outs, first, product, slots, tags):
    me = lax.axis_index("dom")
    row_at = lax.broadcasted_iota(I32, (TAG_ROWS, product.shape[2]), 0)
    for relative, out in enumerate(outs, first):
        target = me ^ relative
        marks = jnp.zeros((TAG_ROWS, product.shape[2]), F32)
        for place in range(CAP):
            number = slots[target * CAP + place]
            marks = jnp.where(row_at == place, tags[target * CAP + place].astype(F32), marks)

            @pl.when(number >= 0)
            def _():
                out[block_at(place), :] = product[number]

        out[PAIR:, :] = marks.astype(BF16)


def push_far_kernel(half, src_hbm, part_hbm, dst_hbm, feat_hbm, tiles_hbm, *refs):
    outs, (product, slots, tags) = refs[:half], refs[half : half + 3]
    src, part, dst, feat, tiles, count, sems = refs[half + 3 :]
    pairs = [
        (part_hbm, part),
        (dst_hbm, dst),
        (src_hbm, src),
        (feat_hbm, feat),
        (tiles_hbm, tiles),
    ]
    copies = [
        pltpu.make_async_copy(source, target, sems.at[number])
        for number, (source, target) in enumerate(pairs)
    ]
    for copy in copies:
        copy.start()
    copies[0].wait()
    copies[1].wait()
    fill_slots(part, count, slots, tiles.shape[0])
    for place in range(slots.shape[0]):
        number = slots[place]
        tags[place] = jnp.where(number >= 0, dst[jnp.maximum(number, 0)] + 1, 0)
    for copy in copies[2:]:
        copy.wait()
    for number in range(tiles.shape[0]):
        product[number] = dot_tn(tiles[number], feat[src[number]]).astype(BF16)
    place_tiles(outs, half, product, slots, tags)


def push_near_kernel(product, slots, tags, *outs):
    place_tiles(outs, 0, product, slots, tags)


def local_kernel(src, dst, feat, tiles, out):
    out[...] = jnp.zeros(out.shape, F32)
    for number in range(tiles.shape[0]):
        out[dst[number]] += dot_tn(tiles[number], feat[src[number]])


def rotate_kernel(first, second, out_first, out_second):
    shards = lax.axis_size("chan")
    me = lax.axis_index("chan")
    width = first.shape[1] // shards
    for own in range(shards):

        @pl.when(me == own)
        def _():
            cut = own * width
            for source, out in ((first, out_first), (second, out_second)):
                out[:, : source.shape[1] - cut] = source[:, cut:]
                if cut:
                    out[:, source.shape[1] - cut :] = source[:, :cut]


def read_tags(pairs, blocks, got):
    channels = pairs[0].shape[1]
    bits = blocks.bit_length()
    per_word = max(1, 24 // (bits * CAP))
    row_at = lax.broadcasted_iota(I32, (TAG_ROWS, channels), 0)
    unit = jnp.zeros((TAG_ROWS, channels), F32)
    for place in range(CAP):
        unit = jnp.where(row_at == place, float(1 << (bits * place)), unit)
    for first in range(0, len(pairs), per_word):
        members = range(first, min(first + per_word, len(pairs)))
        word = jnp.zeros((TAG_ROWS, channels), F32)
        for member in members:
            scale = float(1 << (bits * CAP * (member - first)))
            word = word + pairs[member][PAIR:, :].astype(F32) * (unit * scale)
        packed = jnp.max(jnp.sum(word, axis=0, keepdims=True)).astype(I32)
        for member in members:
            for place in range(CAP):
                shift = bits * (CAP * (member - first) + place)
                got[member * CAP + place] = ((packed >> shift) & (2**bits - 1)) - 1


def add_pairs(pairs, got, acc):
    for number, pair in enumerate(pairs):
        for place in range(CAP):
            block = got[number * CAP + place]

            @pl.when(block >= 0)
            def _():
                acc[block] += pair[block_at(place), :].astype(F32)


def relay_kernel(*refs):
    pairs, (dense, got, acc) = refs[:-3], refs[-3:]
    read_tags(pairs, acc.shape[0], got)
    acc[...] = jnp.zeros(acc.shape, F32)
    add_pairs(pairs, got, acc)
    dense[...] = acc[...].astype(BF16)


def mid_kernel(half, shards, *refs):
    pairs, rest = refs[:half], refs[half:]
    dense, local, feat, w_self, w_neigh, degrees, averaged = rest[:7]
    shares, (got, acc) = rest[7 : 7 + shards], rest[7 + shards :]
    read_tags(pairs, acc.shape[0], got)
    acc[...] = local[...] + dense[...].astype(F32)
    add_pairs(pairs, got, acc)
    divisor = degree_columns(degrees)
    width = shares[0].shape[1]
    for block in range(acc.shape[0]):
        at = block_at(block)
        mean = (acc[block] / divisor[:, block : block + 1]).astype(BF16)
        averaged[at, :] = mean
        value = dot_nn(feat[block], w_self[...]) + dot_nn(mean, w_neigh[...])
        value = value.astype(BF16)
        for piece, share in enumerate(shares):
            share[at, :] = value[:, piece * width : (piece + 1) * width]


def silu_kernel(*refs):
    shares, cotangent, output, slopes = refs[:-3], refs[-3], refs[-2], refs[-1]
    for block in range(output.shape[0] // TILE):
        at = block_at(block)
        value = shares[0][at, :].astype(F32)
        for piece in shares[1:]:
            value = value + piece[at, :].astype(F32)
        gate = 1.0 / (1.0 + jnp.exp(-value))
        output[at, :] = (value * gate).astype(BF16)
        slope = gate * (1.0 + value * (1.0 - gate))
        slopes[at, :] = (cotangent[at, :].astype(F32) * slope).astype(BF16)


def slopes_times(slopes, weights, at):
    width = slopes[0].shape[1]
    total = dot_nt(slopes[0][at, :], weights[:, :width])
    for piece in range(1, len(slopes)):
        columns = slice(piece * width, (piece + 1) * width)
        total = total + dot_nt(slopes[piece][at, :], weights[:, columns])
    return total


def back_kernel(w_neigh, degrees, *refs):
    slopes, back = refs[:-1], refs[-1]
    divisor = degree_columns(degrees)
    for block in range(back.shape[0]):
        total = slopes_times(slopes, w_neigh, block_at(block))
        back[block] = (total / divisor[:, block : block + 1]).astype(BF16)


def spread_kernel(got, rows, *outs):
    for number, out in enumerate(outs, 1):
        for place in range(CAP):
            block = got[number * CAP + place]

            @pl.when(block >= 0)
            def _():
                out[block_at(place), :] = rows[block]


def grads_kernel(inner, feat, averaged, *refs):
    shards = lax.axis_size("chan")
    slopes, outs, whole = refs[:shards], refs[shards:-1], refs[-1]
    channels = feat.shape[1]
    width = slopes[0].shape[1]
    for piece, slope in enumerate(slopes):
        columns = slice(piece * width, (piece + 1) * width)
        whole[:channels, columns] = dot_tn(feat[...], slope[...])
        whole[channels:, columns] = dot_tn(averaged[...], slope[...])
    me = lax.axis_index("dom") & (inner - 1)
    rows = outs[0].shape[0]
    for relative, out in enumerate(outs):
        for owner in range(inner):

            @pl.when((me ^ relative) == owner)
            def _():
                out[...] = whole[owner * rows : (owner + 1) * rows, :].astype(out.dtype)


def gather_sum_kernel(*refs):
    parts, out = refs[:-1], refs[-1]
    total = parts[0][...].astype(F32)
    for part in parts[1:]:
        total = total + part[...].astype(F32)
    out[...] = total.astype(BF16)


def place_rows(parts, out):
    me = lax.axis_index("dom") & (len(parts) - 1)
    rows = parts[0].shape[0]
    for relative, part in enumerate(parts):
        for owner in range(len(parts)):

            @pl.when((me ^ relative) == owner)
            def _():
                out[owner * rows : (owner + 1) * rows, :] = part[...]


def finish_grads_kernel(scale, *refs):
    parts, outs, whole = refs[:-3], refs[-3:-1], refs[-1]
    place_rows(parts, whole)
    shards = lax.axis_size("chan")
    me = lax.axis_index("chan")
    columns = whole.shape[1]
    channels = outs[0].shape[0]
    for own in range(shards):

        @pl.when(me == own)
        def _():
            cut = own * (columns // shards)
            for number, out in enumerate(outs):
                rows = slice(number * channels, (number + 1) * channels)
                out[:, cut:] = whole[rows, : columns - cut].astype(F32) * scale
                if cut:
                    out[:, :cut] = whole[rows, columns - cut :].astype(F32) * scale


def local_back_kernel(src, dst, tiles, back, w_self, *refs):
    slopes, out = refs[:-1], refs[-1]
    for block in range(out.shape[0]):
        out[block] = slopes_times(slopes, w_self, block_at(block))
    for number in range(tiles.shape[0]):
        out[src[number]] += dot_nn(tiles[number], back[dst[number]])


def final_kernel(half, src, dst, slots, tiles, back, far, partial, *refs):
    near_rows, far_rows = refs[: half - 1], refs[half - 1 : 2 * half - 2]
    out, rows, acc = refs[2 * half - 2 :]
    me = lax.axis_index("dom")
    for relative in range(2 * half):
        target = me ^ relative
        shift = relative % half
        for place in range(CAP):
            number = slots[target * CAP + place]

            @pl.when(number >= 0)
            def _():
                if shift:
                    arrived = (near_rows if relative < half else far_rows)[shift - 1]
                    rows[number] = arrived[block_at(place), :]
                else:
                    held = back if relative < half else far
                    rows[number] = held[dst[number]]

    acc[...] = partial[...]
    for number in range(tiles.shape[0]):
        acc[src[number]] += dot_nn(tiles[number], rows[number])
    out[...] = acc[...].astype(BF16)


def swap(value, relative):
    count = lax.axis_size("dom")
    pairs = [(at, at ^ relative) for at in range(count)]
    return lax.ppermute(value, "dom", pairs)


def swap_all(values, first):
    out = [values[0]] + [None] * (len(values) - 1)
    for k in range(len(values) - 1, 0, -1):
        out[k] = swap(values[k], k * first)
    return out


def around(value, shift):
    count = lax.axis_size("chan")
    return lax.ppermute(value, "chan", [(at, (at + shift) % count) for at in range(count)])


def per_device(
    features,
    w_self,
    w_neigh,
    degrees,
    local_src,
    local_dst,
    local_tiles,
    remote_src,
    remote_part,
    remote_dst,
    remote_tiles,
    cotangent,
):
    domains = lax.axis_size("dom")
    shards = lax.axis_size("chan")
    node_rows, channels = features.shape
    out_width = w_self.shape[1]
    own_width = out_width // shards
    blocks = node_rows // TILE
    n_remote = remote_tiles.shape[0]
    half = domains // 2
    early = max(1, half // 2)
    inner, outer_bits = inner_and_outer(domains)
    feat_blocks = features.reshape(blocks, TILE, channels)
    degree_rows = degrees.reshape(blocks, TILE)
    targets = remote_part[:, 0]
    block_shape = (blocks, TILE, channels)
    product_shape = (n_remote, TILE, channels)
    pair_shape = shape((PAIR + TAG_ROWS, channels), BF16)
    slot_shape = shape((domains * CAP,), I32)
    got_shape = shape((half * CAP,), I32)

    pushed = call(
        lambda *refs: push_far_kernel(half, *refs),
        [(VMEM, pair_shape)] * half
        + [(VMEM, shape(product_shape, BF16)), (SMEM, slot_shape), (SMEM, slot_shape)],
        [(HBM, a) for a in (remote_src, targets, remote_dst, feat_blocks, remote_tiles)],
        [pltpu.SMEM((n_remote,), I32)] * 3
        + [
            pltpu.VMEM(block_shape, BF16),
            pltpu.VMEM(remote_tiles.shape, BF16),
            pltpu.SMEM((domains,), I32),
            pltpu.SemaphoreType.DMA((5,)),
        ],
        limit=None,
    )
    far, (product, slots, tags) = pushed[:half], pushed[half:]
    relayed = swap_all(far, 1)
    near = call(
        push_near_kernel, [(VMEM, pair_shape)] * half, vmem([product]) + smem([slots, tags])
    )
    near_early = swap_all(near[:early], 1)

    (local,) = call(
        local_kernel,
        [(VMEM, shape(block_shape, F32))],
        smem([local_src, local_dst]) + vmem([feat_blocks, local_tiles]),
    )
    own_self, own_neigh = call(
        rotate_kernel, [(VMEM, shape(w_self.shape, BF16))] * 2, vmem([w_self, w_neigh])
    )
    dense, got_far = call(
        relay_kernel,
        [(VMEM, shape(block_shape, BF16)), (SMEM, got_shape)],
        vmem(relayed),
        [pltpu.VMEM(block_shape, F32)],
    )
    crossed = swap(dense, half)
    near_late = [None] * (half - early)
    for k in range(half - 1, early - 1, -1):
        near_late[k - early] = swap(near[k], k)
    direct = near_early + near_late

    mids = call(
        lambda *refs: mid_kernel(half, shards, *refs),
        [(VMEM, shape((node_rows, channels), BF16))]
        + [(VMEM, shape((node_rows, own_width), BF16))] * shards
        + [(SMEM, got_shape)],
        vmem(direct + [crossed, local, feat_blocks, own_self, own_neigh, degree_rows]),
        [pltpu.VMEM(block_shape, F32)],
    )
    averaged, shares, got_near = mids[0], mids[1 : 1 + shards], mids[-1]
    pieces = [shares[0]] + [around(shares[k], k) for k in range(1, shards)]
    output, slopes_own = call(
        silu_kernel, [(VMEM, shape((node_rows, own_width), BF16))] * 2, vmem(pieces + [cotangent])
    )
    slopes = [slopes_own] + [around(slopes_own, shards - k) for k in range(1, shards)]

    (back,) = call(
        back_kernel, [(VMEM, shape(block_shape, BF16))], vmem([own_neigh, degree_rows] + slopes)
    )
    back_far = swap(back, half)
    returning = shape((PAIR, channels), BF16)
    near_out = call(
        spread_kernel, [(VMEM, returning)] * (half - 1), [(SMEM, got_near), (VMEM, back)]
    )
    near_back = swap_all([None, *near_out], 1)[1:]

    rows_inner = 2 * channels // inner
    terms = call(
        lambda *refs: grads_kernel(inner, *refs),
        [(VMEM, shape((rows_inner, out_width), F32))]
        + [(VMEM, shape((rows_inner, out_width), BF16))] * (inner - 1),
        vmem([features, averaged] + slopes),
        [pltpu.VMEM((2 * channels, out_width), F32)],
    )
    part_shape = shape((rows_inner, out_width), BF16)
    (total,) = call(gather_sum_kernel, [(VMEM, part_shape)], vmem(swap_all(terms, 1)))
    for bit in range(outer_bits):
        arrived = swap(total, inner << bit)
        (total,) = call(gather_sum_kernel, [(VMEM, part_shape)], vmem([total, arrived]))
    totals = swap_all([total] * inner, 1)
    scale = 1.0 / math.sqrt(float(node_rows * domains))
    grad_self, grad_neigh = call(
        lambda *refs: finish_grads_kernel(scale, *refs),
        [(VMEM, shape((channels, out_width), F32))] * 2,
        vmem(totals),
        [pltpu.VMEM((2 * channels, out_width), BF16)],
    )

    far_out = call(
        spread_kernel, [(VMEM, returning)] * (half - 1), [(SMEM, got_far), (VMEM, back_far)]
    )
    far_back = swap_all([None, *far_out], 1)[1:]
    (partial,) = call(
        local_back_kernel,
        [(VMEM, shape(block_shape, F32))],
        smem([local_src, local_dst]) + vmem([local_tiles, back, own_self] + slopes),
    )
    (grad_features,) = call(
        lambda *refs: final_kernel(half, *refs),
        [(VMEM, shape(block_shape, BF16))],
        smem([remote_src, remote_dst, slots])
        + vmem([remote_tiles, back, back_far, partial] + near_back + far_back),
        [pltpu.VMEM(product_shape, BF16), pltpu.VMEM(block_shape, F32)],
    )
    return (output, grad_self, grad_neigh, grad_features.reshape(node_rows, channels))


def inner_and_outer(domains):
    inner_bits = domains.bit_length() // 2
    return 1 << inner_bits, domains.bit_length() - 1 - inner_bits


def solution(mesh):
    in_specs = (
        P("dom", "chan"),
        P("chan", None),
        P("chan", None),
        P("dom"),
        P("dom"),
        P("dom"),
        P("dom", None, None),
        P("dom"),
        P("dom", None),
        P("dom"),
        P("dom", None, None),
        P("dom", "chan"),
    )
    out_specs = (P("dom", "chan"), P("chan", None), P("chan", None), P("dom", "chan"))
    return jax.shard_map(
        per_device, mesh=mesh, in_specs=in_specs, out_specs=out_specs, check_vma=False
    )
```

profile of v0, /device:TPU:0, one launch (start us, length us, event | category | flops | bytes accessed | tf_op | source)
XLA Modules:
  0.0 128.1 jit_solution(16216709392532571095)
XLA Ops:
  0.6 3.3 %shard_map.147 = (bf16[264,256]{1,0:T(8,128)(2,1)}, bf16[264,256]{1,0:T(8,128)(2,1)}, bf16[264,256]{1,0:T(8,128)(2,1)}, bf16[264,256]{1,0:T(8,128)(2,1)}, bf16[2...) custom-call(s32[16]{0:T(128)} %refs_0_.5, ...), custom_call_target="tpu_custom_call" | custom-call | flops 1048576 | bytes 1048576 | tf_op jit(solution)/shard_map/pallas_call | solution.py:29
  3.9 3.0 %collective-permute-start.7 = (bf16[264,256]{1,0:T(8,128)(2,1)}, bf16[264,256]{1,0:T(8,128)(2,1)S(1)}, u32[]{:S(2)}, u32[]{:S(2)}) collective-permute-start(bf16[264,256]{1,0:T(8,128)(2,1)} %get-tuple-element.65), channel_id=1, source_target_pairs={{0,2},{2,0},{4,6},{6,4},{8,10},{10,8},{12,14},{14,12},{16,18},{18,... | collective-permute-start | bytes 405512 | tf_op jit(solution)/shard_map/ppermute | solution.py:342
  8.5 2.0 %collective-permute-start.10 = (bf16[264,256]{1,0:T(8,128)(2,1)}, bf16[264,256]{1,0:T(8,128)(2,1)S(1)}, u32[]{:S(2)}, u32[]{:S(2)}) collective-permute-start(bf16[264,256]{1,0:T(8,128)(2,1)} %get-tuple-element.68), channel_id=1, source_target_pairs={{0,8},{2,10},{4,12},{6,14},{8,0},{10,2},{12,4},{14,6},{16,24},{18,... | collective-permute-start | bytes 405512 | tf_op jit(solution)/shard_map/ppermute | solution.py:342
  11.9 2.5 %collective-permute-start.12 = (bf16[264,256]{1,0:T(8,128)(2,1)}, bf16[264,256]{1,0:T(8,128)(2,1)S(1)}, u32[]{:S(2)}, u32[]{:S(2)}) collective-permute-start(bf16[264,256]{1,0:T(8,128)(2,1)} %get-tuple-element.70), channel_id=1, source_target_pairs={{0,12},{2,14},{4,8},{6,10},{8,4},{10,6},{12,0},{14,2},{16,28},{18,... | collective-permute-start | bytes 405512 | tf_op jit(solution)/shard_map/ppermute | solution.py:342
  16.2 3.2 %collective-permute-done.11.refs_5_ = bf16[264,256]{1,0:T(8,128)(2,1)S(1)} collective-permute-done((bf16[264,256]{1,0:T(8,128)(2,1)}, bf16[264,256]{1,0:T(8,128)(2,1)S(1)}, u32[]{:S(2)}, u32[]{:S(2)}) %collective-permute-start.11) | collective-permute-done | bytes 135200 | tf_op jit(solution)/shard_map/ppermute | solution.py:342
  19.4 2.9 %collective-permute-done.12.refs_6_ = bf16[264,256]{1,0:T(8,128)(2,1)S(1)} collective-permute-done((bf16[264,256]{1,0:T(8,128)(2,1)}, bf16[264,256]{1,0:T(8,128)(2,1)S(1)}, u32[]{:S(2)}, u32[]{:S(2)}) %collective-permute-start.12) | collective-permute-done | bytes 135200 | tf_op jit(solution)/shard_map/ppermute | solution.py:342
  22.3 1.9 %collective-permute-done.13.refs_7_ = bf16[264,256]{1,0:T(8,128)(2,1)S(1)} collective-permute-done((bf16[264,256]{1,0:T(8,128)(2,1)}, bf16[264,256]{1,0:T(8,128)(2,1)S(1)}, u32[]{:S(2)}, u32[]{:S(2)}) %collective-permute-start.13) | collective-permute-done | bytes 135200 | tf_op jit(solution)/shard_map/ppermute | solution.py:342
  26.1 2.6 %collective-permute-start.14 = (bf16[8,128,256]{2,1,0:T(8,128)(2,1)S(1)}, bf16[8,128,256]{2,1,0:T(8,128)(2,1)S(1)}, u32[]{:S(2)}, u32[]{:S(2)}) collective-permute-start(bf16[8,128,256]{2,1,0:T(8,128)(2,1)S(1)} %get-tuple-element.72), channel_id=1, source_target_pairs={{0,16},{2,18},{4,20},{6,22},{8,24},{10,26},{12,28},{14,30},{16,0},... | collective-permute-start | bytes 1572872 | tf_op jit(solution)/shard_map/ppermute | solution.py:342
  32.0 1.8 %collective-permute-start.2 = (bf16[264,256]{1,0:T(8,128)(2,1)S(1)}, bf16[264,256]{1,0:T(8,128)(2,1)S(1)}, u32[]{:S(2)}, u32[]{:S(2)}) collective-permute-start(bf16[264,256]{1,0:T(8,128)(2,1)S(1)} %get-tuple-element.59), channel_id=1, source_target_pairs={{0,6},{2,4},{4,2},{6,0},{8,14},{10,12},{12,10},{14,8},{16,22},{18,... | collective-permute-start | bytes 405512 | tf_op jit(solution)/shard_map/ppermute | solution.py:342
  35.3 2.0 %collective-permute-done.refs_1_ = bf16[264,256]{1,0:T(8,128)(2,1)S(1)} collective-permute-done((bf16[264,256]{1,0:T(8,128)(2,1)S(1)}, bf16[264,256]{1,0:T(8,128)(2,1)S(1)}, u32[]{:S(2)}, u32[]{:S(2)}) %collective-permute-start) | collective-permute-done | bytes 135200 | tf_op jit(solution)/shard_map/ppermute | solution.py:342
  41.7 8.5 %collective-permute-done.3.refs_4_ = bf16[264,256]{1,0:T(8,128)(2,1)S(1)} collective-permute-done((bf16[264,256]{1,0:T(8,128)(2,1)S(1)}, bf16[264,256]{1,0:T(8,128)(2,1)S(1)}, u32[]{:S(2)}, u32[]{:S(2)}) %collective-permute-start.3) | collective-permute-done | bytes 135200 | tf_op jit(solution)/shard_map/ppermute | solution.py:342
  50.2 4.1 %collective-permute-done.4.refs_5_ = bf16[264,256]{1,0:T(8,128)(2,1)S(1)} collective-permute-done((bf16[264,256]{1,0:T(8,128)(2,1)S(1)}, bf16[264,256]{1,0:T(8,128)(2,1)S(1)}, u32[]{:S(2)}, u32[]{:S(2)}) %collective-permute-start.4) | collective-permute-done | bytes 135200 | tf_op jit(solution)/shard_map/ppermute | solution.py:342
  55.2 2.1 %collective-permute-done.6.refs_7_ = bf16[264,256]{1,0:T(8,128)(2,1)S(1)} collective-permute-done((bf16[264,256]{1,0:T(8,128)(2,1)S(1)}, bf16[264,256]{1,0:T(8,128)(2,1)S(1)}, u32[]{:S(2)}, u32[]{:S(2)}) %collective-permute-start.6) | collective-permute-done | bytes 135200 | tf_op jit(solution)/shard_map/ppermute | solution.py:342
  58.8 1.9 %collective-permute-done.15.refs_1_ = bf16[1024,256]{1,0:T(8,128)(2,1)S(1)} collective-permute-done((bf16[1024,256]{1,0:T(8,128)(2,1)S(1)}, bf16[1024,256]{1,0:T(8,128)(2,1)S(1)}, u32[]{:S(2)}, u32[]{:S(2)}) %collective-permute-start.15) | collective-permute-done | bytes 524320 | tf_op jit(solution)/shard_map/ppermute | solution.py:354
  62.0 1.8 %collective-permute-done.16.refs_3_.refs_1_ = bf16[1024,256]{1,0:T(8,128)(2,1)S(1)} collective-permute-done((bf16[1024,256]{1,0:T(8,128)(2,1)S(1)}, bf16[1024,256]{1,0:T(8,128)(2,1)S(1)}, u32[]{:S(2)}, u32[]{:S(2)}) %collective-permute-start.16) | collective-permute-done | bytes 524320 | tf_op jit(solution)/shard_map/ppermute | solution.py:354
  70.6 1.8 %collective-permute-done.18.refs_2_ = bf16[128,512]{1,0:T(8,128)(2,1)S(1)} collective-permute-done((bf16[128,512]{1,0:T(8,128)(2,1)S(1)}, bf16[128,512]{1,0:T(8,128)(2,1)S(1)}, u32[]{:S(2)}, u32[]{:S(2)}) %collective-permute-start.18) | collective-permute-done | bytes 131104 | tf_op jit(solution)/shard_map/ppermute | solution.py:342
  79.4 2.3 %collective-permute-done.20.refs_1_ = bf16[128,512]{1,0:T(8,128)(2,1)S(1)} collective-permute-done((bf16[128,512]{1,0:T(8,128)(2,1)S(1)}, bf16[128,512]{1,0:T(8,128)(2,1)S(1)}, u32[]{:S(2)}, u32[]{:S(2)}) %collective-permute-start.20) | collective-permute-done | bytes 131104 | tf_op jit(solution)/shard_map/ppermute | solution.py:342
  81.8 2.0 %collective-permute-start.21 = (bf16[128,512]{1,0:T(8,128)(2,1)S(1)}, bf16[128,512]{1,0:T(8,128)(2,1)S(1)}, u32[]{:S(2)}, u32[]{:S(2)}) collective-permute-start(bf16[128,512]{1,0:T(8,128)(2,1)S(1)} %shard_map.156.refs_0_), channel_id=1, source_target_pairs={{0,16},{2,18},{4,20},{6,22},{8,24},{10,26},{12,28},{14,30},{16,0},... | collective-permute-start | bytes 393224 | tf_op jit(solution)/shard_map/ppermute | solution.py:342
  87.3 9.9 %collective-permute-done.21.refs_1_ = bf16[128,512]{1,0:T(8,128)(2,1)S(1)} collective-permute-done((bf16[128,512]{1,0:T(8,128)(2,1)S(1)}, bf16[128,512]{1,0:T(8,128)(2,1)S(1)}, u32[]{:S(2)}, u32[]{:S(2)}) %collective-permute-start.21) | collective-permute-done | bytes 131104 | tf_op jit(solution)/shard_map/ppermute | solution.py:342
  102.4 3.6 %collective-permute-done.31.refs_12_ = bf16[256,256]{1,0:T(8,128)(2,1)S(1)} collective-permute-done((bf16[256,256]{1,0:T(8,128)(2,1)S(1)}, bf16[256,256]{1,0:T(8,128)(2,1)S(1)}, u32[]{:S(2)}, u32[]{:S(2)}) %collective-permute-start.31) | collective-permute-done | bytes 131104 | tf_op jit(solution)/shard_map/ppermute | solution.py:342
  114.9 1.8 %collective-permute-done.34.refs_15_ = bf16[256,256]{1,0:T(8,128)(2,1)S(1)} collective-permute-done((bf16[256,256]{1,0:T(8,128)(2,1)S(1)}, bf16[256,256]{1,0:T(8,128)(2,1)S(1)}, u32[]{:S(2)}, u32[]{:S(2)}) %collective-permute-start.34) | collective-permute-done | bytes 131104 | tf_op jit(solution)/shard_map/ppermute | solution.py:342
  121.1 2.9 %collective-permute-done.38.refs_19_ = bf16[256,256]{1,0:T(8,128)(2,1)S(1)} collective-permute-done((bf16[256,256]{1,0:T(8,128)(2,1)S(1)}, bf16[256,256]{1,0:T(8,128)(2,1)S(1)}, u32[]{:S(2)}, u32[]{:S(2)}) %collective-permute-start.38) | collective-permute-done | bytes 131104 | tf_op jit(solution)/shard_map/ppermute | solution.py:342
  124.0 1.9 %collective-permute-done.39.refs_20_ = bf16[256,256]{1,0:T(8,128)(2,1)S(1)} collective-permute-done((bf16[256,256]{1,0:T(8,128)(2,1)S(1)}, bf16[256,256]{1,0:T(8,128)(2,1)S(1)}, u32[]{:S(2)}, u32[]{:S(2)}) %collective-permute-start.39) | collective-permute-done | bytes 131104 | tf_op jit(solution)/shard_map/ppermute | solution.py:342
  126.0 2.2 %shard_map.163 = bf16[8,128,256]{2,1,0:T(8,128)(2,1)} custom-call(s32[16]{0:T(128)S(1)} %copy-done.12, s32[16]{0:T(128)S(1)} %copy-done.13, s32[32]{0:T(128)S(1)} %copy-done.9, bf16[16,128,128]{2,1,0:T(8,128)(2,1)S(1)} %copy-done.1, bf16[8,128,256]{2,1,0:T(8,128)(2,1)S(1)} %shard_map.159.back.rows.refs_4_, ...), custom_call_target="tpu_custom_call" | custom-call | flops 1048576 | bytes 1048576 | tf_op jit(solution)/shard_map/pallas_call | solution.py:29
  (103 shorter events, 55.3 us)
Async XLA Ops:
  10.5 8.9 %collective-permute-start.11 = (bf16[264,256]{1,0:T(8,128)(2,1)}, bf16[264,256]{1,0:T(8,128)(2,1)S(1)}, u32[]{:S(2)}, u32[]{:S(2)}) collective-permute-start(bf16[264,256]{1,0:T(8,128)(2,1)} %get-tuple-element.69), channel_id=1, source_target_pairs={{0,10},{2,8},{4,14},{6,12},{8,2},{10,0},{12,6},{14,4},{16,26},{18,... | collective-permute-start | bytes 405512 | tf_op jit(solution)/shard_map/ppermute | solution.py:342
  11.9 10.4 %collective-permute-start.12 = (bf16[264,256]{1,0:T(8,128)(2,1)}, bf16[264,256]{1,0:T(8,128)(2,1)S(1)}, u32[]{:S(2)}, u32[]{:S(2)}) collective-permute-start(bf16[264,256]{1,0:T(8,128)(2,1)} %get-tuple-element.70), channel_id=1, source_target_pairs={{0,12},{2,14},{4,8},{6,10},{8,4},{10,6},{12,0},{14,2},{16,28},{18,... | collective-permute-start | bytes 405512 | tf_op jit(solution)/shard_map/ppermute | solution.py:342
  14.4 9.8 %collective-permute-start.13 = (bf16[264,256]{1,0:T(8,128)(2,1)}, bf16[264,256]{1,0:T(8,128)(2,1)S(1)}, u32[]{:S(2)}, u32[]{:S(2)}) collective-permute-start(bf16[264,256]{1,0:T(8,128)(2,1)} %get-tuple-element.71), channel_id=1, source_target_pairs={{0,14},{2,12},{4,10},{6,8},{8,6},{10,4},{12,2},{14,0},{16,30},{18,... | collective-permute-start | bytes 405512 | tf_op jit(solution)/shard_map/ppermute | solution.py:342
  26.1 31.2 %collective-permute-start.14 = (bf16[8,128,256]{2,1,0:T(8,128)(2,1)S(1)}, bf16[8,128,256]{2,1,0:T(8,128)(2,1)S(1)}, u32[]{:S(2)}, u32[]{:S(2)}) collective-permute-start(bf16[8,128,256]{2,1,0:T(8,128)(2,1)S(1)} %get-tuple-element.72), channel_id=1, source_target_pairs={{0,16},{2,18},{4,20},{6,22},{8,24},{10,26},{12,28},{14,30},{16,0},... | collective-permute-start | bytes 1572872 | tf_op jit(solution)/shard_map/ppermute | solution.py:342
  33.7 16.5 %collective-permute-start.3 = (bf16[264,256]{1,0:T(8,128)(2,1)S(1)}, bf16[264,256]{1,0:T(8,128)(2,1)S(1)}, u32[]{:S(2)}, u32[]{:S(2)}) collective-permute-start(bf16[264,256]{1,0:T(8,128)(2,1)S(1)} %get-tuple-element.60), channel_id=1, source_target_pairs={{0,8},{2,10},{4,12},{6,14},{8,0},{10,2},{12,4},{14,6},{16,24},{18,... | collective-permute-start | bytes 405512 | tf_op jit(solution)/shard_map/ppermute | solution.py:342
  37.3 17.0 %collective-permute-start.4 = (bf16[264,256]{1,0:T(8,128)(2,1)S(1)}, bf16[264,256]{1,0:T(8,128)(2,1)S(1)}, u32[]{:S(2)}, u32[]{:S(2)}) collective-permute-start(bf16[264,256]{1,0:T(8,128)(2,1)S(1)} %get-tuple-element.61), channel_id=1, source_target_pairs={{0,10},{2,8},{4,14},{6,12},{8,2},{10,0},{12,6},{14,4},{16,26},{18,... | collective-permute-start | bytes 405512 | tf_op jit(solution)/shard_map/ppermute | solution.py:342
  37.4 17.9 %collective-permute-start.5 = (bf16[264,256]{1,0:T(8,128)(2,1)S(1)}, bf16[264,256]{1,0:T(8,128)(2,1)S(1)}, u32[]{:S(2)}, u32[]{:S(2)}) collective-permute-start(bf16[264,256]{1,0:T(8,128)(2,1)S(1)} %get-tuple-element.62), channel_id=1, source_target_pairs={{0,12},{2,14},{4,8},{6,10},{8,4},{10,6},{12,0},{14,2},{16,28},{18,... | collective-permute-start | bytes 405512 | tf_op jit(solution)/shard_map/ppermute | solution.py:342
  39.4 17.9 %collective-permute-start.6 = (bf16[264,256]{1,0:T(8,128)(2,1)S(1)}, bf16[264,256]{1,0:T(8,128)(2,1)S(1)}, u32[]{:S(2)}, u32[]{:S(2)}) collective-permute-start(bf16[264,256]{1,0:T(8,128)(2,1)S(1)} %get-tuple-element.63), channel_id=1, source_target_pairs={{0,14},{2,12},{4,10},{6,8},{8,6},{10,4},{12,2},{14,0},{16,30},{18,... | collective-permute-start | bytes 405512 | tf_op jit(solution)/shard_map/ppermute | solution.py:342
  67.6 31.8 %collective-permute-start.25 = (bf16[8,128,256]{2,1,0:T(8,128)(2,1)S(1)}, bf16[8,128,256]{2,1,0:T(8,128)(2,1)S(1)}, u32[]{:S(2)}, u32[]{:S(2)}) collective-permute-start(bf16[8,128,256]{2,1,0:T(8,128)(2,1)S(1)} %shard_map.159.back.rows.refs_4_), channel_id=1, source_target_pairs={{0,16},{2,18},{4,20},{6,22},{8,24},{10,26},{12,28},{14,30},{16,0},... | collective-permute-start | bytes 1572872 | tf_op jit(solution)/shard_map/ppermute | solution.py:342
  81.8 15.4 %collective-permute-start.21 = (bf16[128,512]{1,0:T(8,128)(2,1)S(1)}, bf16[128,512]{1,0:T(8,128)(2,1)S(1)}, u32[]{:S(2)}, u32[]{:S(2)}) collective-permute-start(bf16[128,512]{1,0:T(8,128)(2,1)S(1)} %shard_map.156.refs_0_), channel_id=1, source_target_pairs={{0,16},{2,18},{4,20},{6,22},{8,24},{10,26},{12,28},{14,30},{16,0},... | collective-permute-start | bytes 393224 | tf_op jit(solution)/shard_map/ppermute | solution.py:342
  83.8 14.3 %collective-permute-start.29 = (bf16[256,256]{1,0:T(8,128)(2,1)S(1)}, bf16[256,256]{1,0:T(8,128)(2,1)S(1)}, u32[]{:S(2)}, u32[]{:S(2)}) collective-permute-start(bf16[256,256]{1,0:T(8,128)(2,1)S(1)} %get-tuple-element.90), channel_id=1, source_target_pairs={{0,8},{2,10},{4,12},{6,14},{8,0},{10,2},{12,4},{14,6},{16,24},{18,... | collective-permute-start | bytes 393224 | tf_op jit(solution)/shard_map/ppermute | solution.py:342
  84.4 16.5 %collective-permute-start.30 = (bf16[256,256]{1,0:T(8,128)(2,1)S(1)}, bf16[256,256]{1,0:T(8,128)(2,1)S(1)}, u32[]{:S(2)}, u32[]{:S(2)}) collective-permute-start(bf16[256,256]{1,0:T(8,128)(2,1)S(1)} %get-tuple-element.91), channel_id=1, source_target_pairs={{0,10},{2,8},{4,14},{6,12},{8,2},{10,0},{12,6},{14,4},{16,26},{18,... | collective-permute-start | bytes 393224 | tf_op jit(solution)/shard_map/ppermute | solution.py:342
  85.9 20.1 %collective-permute-start.31 = (bf16[256,256]{1,0:T(8,128)(2,1)S(1)}, bf16[256,256]{1,0:T(8,128)(2,1)S(1)}, u32[]{:S(2)}, u32[]{:S(2)}) collective-permute-start(bf16[256,256]{1,0:T(8,128)(2,1)S(1)} %get-tuple-element.92), channel_id=1, source_target_pairs={{0,12},{2,14},{4,8},{6,10},{8,4},{10,6},{12,0},{14,2},{16,28},{18,... | collective-permute-start | bytes 393224 | tf_op jit(solution)/shard_map/ppermute | solution.py:342
  97.1 10.3 %collective-permute-start.32 = (bf16[256,256]{1,0:T(8,128)(2,1)S(1)}, bf16[256,256]{1,0:T(8,128)(2,1)S(1)}, u32[]{:S(2)}, u32[]{:S(2)}) collective-permute-start(bf16[256,256]{1,0:T(8,128)(2,1)S(1)} %get-tuple-element.93), channel_id=1, source_target_pairs={{0,14},{2,12},{4,10},{6,8},{8,6},{10,4},{12,2},{14,0},{16,30},{18,... | collective-permute-start | bytes 393224 | tf_op jit(solution)/shard_map/ppermute | solution.py:342
  98.1 11.4 %collective-permute-start.24 = (bf16[128,512]{1,0:T(8,128)(2,1)S(1)}, bf16[128,512]{1,0:T(8,128)(2,1)S(1)}, u32[]{:S(2)}, u32[]{:S(2)}) collective-permute-start(bf16[128,512]{1,0:T(8,128)(2,1)S(1)} %shard_map.157.refs_0_), channel_id=1, source_target_pairs={{0,6},{2,4},{4,2},{6,0},{8,14},{10,12},{12,10},{14,8},{16,22},{18,... | collective-permute-start | bytes 393224 | tf_op jit(solution)/shard_map/ppermute | solution.py:342
  99.4 11.9 %collective-permute-start.23 = (bf16[128,512]{1,0:T(8,128)(2,1)S(1)}, bf16[128,512]{1,0:T(8,128)(2,1)S(1)}, u32[]{:S(2)}, u32[]{:S(2)}) collective-permute-start(bf16[128,512]{1,0:T(8,128)(2,1)S(1)} %shard_map.157.refs_0_), channel_id=1, source_target_pairs={{0,4},{2,6},{4,0},{6,2},{8,12},{10,14},{12,8},{14,10},{16,20},{18,... | collective-permute-start | bytes 393224 | tf_op jit(solution)/shard_map/ppermute | solution.py:342
  100.9 11.5 %collective-permute-start.22 = (bf16[128,512]{1,0:T(8,128)(2,1)S(1)}, bf16[128,512]{1,0:T(8,128)(2,1)S(1)}, u32[]{:S(2)}, u32[]{:S(2)}) collective-permute-start(bf16[128,512]{1,0:T(8,128)(2,1)S(1)} %shard_map.157.refs_0_), channel_id=1, source_target_pairs={{0,2},{2,0},{4,6},{6,4},{8,10},{10,8},{12,14},{14,12},{16,18},{18,... | collective-permute-start | bytes 393224 | tf_op jit(solution)/shard_map/ppermute | solution.py:342
  106.0 8.9 %collective-permute-start.33 = (bf16[256,256]{1,0:T(8,128)(2,1)S(1)}, bf16[256,256]{1,0:T(8,128)(2,1)S(1)}, u32[]{:S(2)}, u32[]{:S(2)}) collective-permute-start(bf16[256,256]{1,0:T(8,128)(2,1)S(1)} %get-tuple-element.95), channel_id=1, source_target_pairs={{0,2},{2,0},{4,6},{6,4},{8,10},{10,8},{12,14},{14,12},{16,18},{18,... | collective-permute-start | bytes 393224 | tf_op jit(solution)/shard_map/ppermute | solution.py:342
  107.5 9.2 %collective-permute-start.34 = (bf16[256,256]{1,0:T(8,128)(2,1)S(1)}, bf16[256,256]{1,0:T(8,128)(2,1)S(1)}, u32[]{:S(2)}, u32[]{:S(2)}) collective-permute-start(bf16[256,256]{1,0:T(8,128)(2,1)S(1)} %get-tuple-element.96), channel_id=1, source_target_pairs={{0,4},{2,6},{4,0},{6,2},{8,12},{10,14},{12,8},{14,10},{16,20},{18,... | collective-permute-start | bytes 393224 | tf_op jit(solution)/shard_map/ppermute | solution.py:342
  109.5 11.1 %collective-permute-start.35 = (bf16[256,256]{1,0:T(8,128)(2,1)S(1)}, bf16[256,256]{1,0:T(8,128)(2,1)S(1)}, u32[]{:S(2)}, u32[]{:S(2)}) collective-permute-start(bf16[256,256]{1,0:T(8,128)(2,1)S(1)} %get-tuple-element.97), channel_id=1, source_target_pairs={{0,6},{2,4},{4,2},{6,0},{8,14},{10,12},{12,10},{14,8},{16,22},{18,... | collective-permute-start | bytes 393224 | tf_op jit(solution)/shard_map/ppermute | solution.py:342
  111.3 9.4 %collective-permute-start.36 = (bf16[256,256]{1,0:T(8,128)(2,1)S(1)}, bf16[256,256]{1,0:T(8,128)(2,1)S(1)}, u32[]{:S(2)}, u32[]{:S(2)}) collective-permute-start(bf16[256,256]{1,0:T(8,128)(2,1)S(1)} %get-tuple-element.98), channel_id=1, source_target_pairs={{0,8},{2,10},{4,12},{6,14},{8,0},{10,2},{12,4},{14,6},{16,24},{18,... | collective-permute-start | bytes 393224 | tf_op jit(solution)/shard_map/ppermute | solution.py:342
  112.4 8.7 %collective-permute-start.37 = (bf16[256,256]{1,0:T(8,128)(2,1)S(1)}, bf16[256,256]{1,0:T(8,128)(2,1)S(1)}, u32[]{:S(2)}, u32[]{:S(2)}) collective-permute-start(bf16[256,256]{1,0:T(8,128)(2,1)S(1)} %get-tuple-element.99), channel_id=1, source_target_pairs={{0,10},{2,8},{4,14},{6,12},{8,2},{10,0},{12,6},{14,4},{16,26},{18,... | collective-permute-start | bytes 393224 | tf_op jit(solution)/shard_map/ppermute | solution.py:342
  114.9 9.1 %collective-permute-start.38 = (bf16[256,256]{1,0:T(8,128)(2,1)S(1)}, bf16[256,256]{1,0:T(8,128)(2,1)S(1)}, u32[]{:S(2)}, u32[]{:S(2)}) collective-permute-start(bf16[256,256]{1,0:T(8,128)(2,1)S(1)} %get-tuple-element.100), channel_id=1, source_target_pairs={{0,12},{2,14},{4,8},{6,10},{8,4},{10,6},{12,0},{14,2},{16,28},{18,... | collective-permute-start | bytes 393224 | tf_op jit(solution)/shard_map/ppermute | solution.py:342
  116.6 9.3 %collective-permute-start.39 = (bf16[256,256]{1,0:T(8,128)(2,1)S(1)}, bf16[256,256]{1,0:T(8,128)(2,1)S(1)}, u32[]{:S(2)}, u32[]{:S(2)}) collective-permute-start(bf16[256,256]{1,0:T(8,128)(2,1)S(1)} %get-tuple-element.101), channel_id=1, source_target_pairs={{0,14},{2,12},{4,10},{6,8},{8,6},{10,4},{12,2},{14,0},{16,30},{18,... | collective-permute-start | bytes 393224 | tf_op jit(solution)/shard_map/ppermute | solution.py:342
  (31 other events, 222.0 us)
where the time goes:
time: 128 us
  waiting for transfers between devices  63.4 us (50%)
  starting transfers between devices  45.8 us (36%)
  Pallas kernels  16.4 us (13%)
  local copies, waits for them, and re-layouts  1.64 us (1%)
    ppermute x38, waiting for transfers between devices, swap(): return lax.ppermute(value, 'dom', pairs)  59.7 us
    ppermute x38, starting transfers between devices, swap(): return lax.ppermute(value, 'dom', pairs)  45.6 us
    pallas_call x17, Pallas kernels, call(): pl.pallas_call(kernel, out_shape=tuple((out for _, out in outs)), in_spec...  16.4 us
    ppermute x2, waiting for transfers between devices, around(): lax.ppermute(value, 'chan', [(at, (at + shift) % count) for at in range(c...  3.67 us
  transfers between devices with their start and end apart: 40, of which 28 were waited for; matrix products, arithmetic and copies ran while one was open for 0% of the time, Pallas kernels for 5%

commit v1 on v0

--- a/solution.py
+++ b/solution.py
@@ -238,17 +238,29 @@
 
 def spread_kernel(got, rows, *outs):
     for number, out in enumerate(outs, 1):
-        for place in range(CAP):
-            block = got[number * CAP + place]
-
-            @pl.when(block >= 0)
-            def _():
-                out[block_at(place), :] = rows[block]
-
-
-def grads_kernel(inner, feat, averaged, *refs):
+        spread_rows(got, rows, number, out)
+
+
+def spread_rows(got, rows, number, out):
+    for place in range(CAP):
+        block = got[number * CAP + place]
+
+        @pl.when(block >= 0)
+        def _():
+            out[block_at(place), :] = rows[block]
+
+
+def extra_pieces(total, holder):
+    rows, width = total.shape
+    channels = holder.shape[1]
+    for piece in range(width // channels):
+        start = PAIR + piece * rows
+        yield slice(piece * channels, (piece + 1) * channels), slice(start, start + rows)
+
+
+def near_terms_kernel(inner, got, back, feat, averaged, *refs):
     shards = lax.axis_size("chan")
-    slopes, outs, whole = refs[:shards], refs[shards:-1], refs[-1]
+    slopes, own, outs, whole = refs[:shards], refs[shards], refs[shards + 1 : -1], refs[-1]
     channels = feat.shape[1]
     width = slopes[0].shape[1]
     for piece, slope in enumerate(slopes):
@@ -256,21 +268,46 @@
         whole[:channels, columns] = dot_tn(feat[...], slope[...])
         whole[channels:, columns] = dot_tn(averaged[...], slope[...])
     me = lax.axis_index("dom") & (inner - 1)
-    rows = outs[0].shape[0]
-    for relative, out in enumerate(outs):
-        for owner in range(inner):
+    rows = own.shape[0]
+    for owner in range(inner):
+        at = slice(owner * rows, (owner + 1) * rows)
+
+        @pl.when(me == owner)
+        def _():
+            own[...] = whole[at, :]
+
+        for relative, out in enumerate(outs, 1):
 
             @pl.when((me ^ relative) == owner)
             def _():
-                out[...] = whole[owner * rows : (owner + 1) * rows, :].astype(out.dtype)
-
-
-def gather_sum_kernel(*refs):
-    parts, out = refs[:-1], refs[-1]
-    total = parts[0][...].astype(F32)
-    for part in parts[1:]:
-        total = total + part[...].astype(F32)
-    out[...] = total.astype(BF16)
+                for columns, places in extra_pieces(own, out):
+                    out[places, :] = whole[at, columns].astype(BF16)
+
+    for relative, out in enumerate(outs, 1):
+        spread_rows(got, back, relative, out)
+
+
+def near_outer_kernel(inner, got, back, own, *refs):
+    arrived, total, outs = refs[: inner - 1], refs[inner - 1], refs[inner:]
+    for columns, places in extra_pieces(total, outs[0]):
+        value = own[:, columns]
+        for part in arrived:
+            value = value + part[places, :].astype(F32)
+        value = value.astype(BF16)
+        total[:, columns] = value
+        outs[0][places, :] = value
+    for relative, out in enumerate(outs, inner):
+        spread_rows(got, back, relative, out)
+
+
+def first_outer_kernel(total, holder, out):
+    for columns, places in extra_pieces(total, holder):
+        value = total[:, columns].astype(F32) + holder[places, :].astype(F32)
+        out[:, columns] = value.astype(BF16)
+
+
+def outer_kernel(total, arrived, out):
+    out[...] = (total[...].astype(F32) + arrived[...].astype(F32)).astype(BF16)
 
 
 def place_rows(parts, out):
@@ -448,24 +485,29 @@
     )
     back_far = swap(back, half)
     returning = shape((PAIR, channels), BF16)
-    near_out = call(
-        spread_kernel, [(VMEM, returning)] * (half - 1), [(SMEM, got_near), (VMEM, back)]
+    rows_inner = 2 * channels // inner
+    loaded = shape((PAIR + rows_inner * out_width // channels, channels), BF16)
+    part_shape = shape((rows_inner, out_width), BF16)
+    own_terms, *near_out = call(
+        lambda *refs: near_terms_kernel(inner, *refs),
+        [(VMEM, shape((rows_inner, out_width), F32))] + [(VMEM, loaded)] * (inner - 1),
+        smem([got_near]) + vmem([back, features, averaged] + slopes),
+        [pltpu.VMEM((2 * channels, out_width), F32)],
     )
     near_back = swap_all([None, *near_out], 1)[1:]
-
-    rows_inner = 2 * channels // inner
-    terms = call(
-        lambda *refs: grads_kernel(inner, *refs),
-        [(VMEM, shape((rows_inner, out_width), F32))]
-        + [(VMEM, shape((rows_inner, out_width), BF16))] * (inner - 1),
-        vmem([features, averaged] + slopes),
-        [pltpu.VMEM((2 * channels, out_width), F32)],
-    )
-    part_shape = shape((rows_inner, out_width), BF16)
-    (total,) = call(gather_sum_kernel, [(VMEM, part_shape)], vmem(swap_all(terms, 1)))
-    for bit in range(outer_bits):
+    total, *near_out = call(
+        lambda *refs: near_outer_kernel(inner, *refs),
+        [(VMEM, part_shape), (VMEM, loaded)] + [(VMEM, returning)] * (half - inner - 1),
+        smem([got_near]) + vmem([back, own_terms] + near_back),
+    )
+    outer_back = [None] * (half - inner)
+    for k in range(half - 1, inner - 1, -1):
+        outer_back[k - inner] = swap(near_out[k - inner], k)
+    near_back = near_back + outer_back
+    (total,) = call(first_outer_kernel, [(VMEM, part_shape)], vmem([total, outer_back[0]]))
+    for bit in range(1, outer_bits):
         arrived = swap(total, inner << bit)
-        (total,) = call(gather_sum_kernel, [(VMEM, part_shape)], vmem([total, arrived]))
+        (total,) = call(outer_kernel, [(VMEM, part_shape)], vmem([total, arrived]))
     totals = swap_all([total] * inner, 1)
     scale = 1.0 / math.sqrt(float(node_rows * domains))
     grad_self, grad_neigh = call(

time: 128 us -> 134 us (1.047)
  waiting for transfers between devices: 63.4 us -> 67.7 us
    ppermute x38 -> x34, waiting for transfers between devices: 59.7 us -> 64 us  [swap(): return lax.ppermute(value, 'dom', pairs)]
    ppermute x38 -> x34, starting transfers between devices: 45.6 us -> 46.3 us  [swap(): return lax.ppermute(value, 'dom', pairs)]
    pallas_call x17 -> x16, Pallas kernels: 16.4 us -> 16.9 us  [call(): pl.pallas_call(kernel, out_shape=tuple((out for _, out in outs)), in_spec...]
  transfers between devices with their start and end apart: 40 -> 36, of which waited for: 28 -> 21; matrix products, arithmetic and copies ran while one was open for 0% -> 0% of each run, Pallas kernels for 5% -> 5%
where the time goes in v1:
time: 134 us
  waiting for transfers between devices  67.7 us (51%)
  starting transfers between devices  46.5 us (35%)
  Pallas kernels  16.9 us (13%)
  local copies, waits for them, and re-layouts  1.62 us (1%)
    ppermute x34, waiting for transfers between devices, swap(): return lax.ppermute(value, 'dom', pairs)  64 us
    ppermute x34, starting transfers between devices, swap(): return lax.ppermute(value, 'dom', pairs)  46.3 us
    pallas_call x16, Pallas kernels, call(): pl.pallas_call(kernel, out_shape=tuple((out for _, out in outs)), in_spec...  16.9 us
    ppermute x2, waiting for transfers between devices, around(): lax.ppermute(value, 'chan', [(at, (at + shift) % count) for at in range(c...  3.67 us
  transfers between devices with their start and end apart: 36, of which 21 were waited for; matrix products, arithmetic and copies ran while one was open for 0% of the time, Pallas kernels for 5%

profile of v1, /device:TPU:0, one launch (start us, length us, event | category | flops | bytes accessed | tf_op | source)
XLA Modules:
  0.0 133.6 jit_solution(8521817787451361561)
XLA Ops:
  0.6 3.2 %shard_map.147 = (bf16[264,256]{1,0:T(8,128)(2,1)}, bf16[264,256]{1,0:T(8,128)(2,1)}, bf16[264,256]{1,0:T(8,128)(2,1)}, bf16[264,256]{1,0:T(8,128)(2,1)}, bf16[2...) custom-call(s32[16]{0:T(128)} %refs_0_.3, ...), custom_call_target="tpu_custom_call" | custom-call | flops 1048576 | bytes 1048576 | tf_op jit(solution)/shard_map/pallas_call | solution.py:29
  3.9 3.1 %collective-permute-start.10 = (bf16[264,256]{1,0:T(8,128)(2,1)}, bf16[264,256]{1,0:T(8,128)(2,1)S(1)}, u32[]{:S(2)}, u32[]{:S(2)}) collective-permute-start(bf16[264,256]{1,0:T(8,128)(2,1)} %get-tuple-element.66), channel_id=1, source_target_pairs={{0,8},{2,10},{4,12},{6,14},{8,0},{10,2},{12,4},{14,6},{16,24},{18,... | collective-permute-start | bytes 405512 | tf_op jit(solution)/shard_map/ppermute | solution.py:379
  8.4 2.5 %collective-permute-start.12 = (bf16[264,256]{1,0:T(8,128)(2,1)}, bf16[264,256]{1,0:T(8,128)(2,1)S(1)}, u32[]{:S(2)}, u32[]{:S(2)}) collective-permute-start(bf16[264,256]{1,0:T(8,128)(2,1)} %get-tuple-element.68), channel_id=1, source_target_pairs={{0,12},{2,14},{4,8},{6,10},{8,4},{10,6},{12,0},{14,2},{16,28},{18,... | collective-permute-start | bytes 405512 | tf_op jit(solution)/shard_map/ppermute | solution.py:379
  10.9 1.9 %collective-permute-start.7 = (bf16[264,256]{1,0:T(8,128)(2,1)}, bf16[264,256]{1,0:T(8,128)(2,1)S(1)}, u32[]{:S(2)}, u32[]{:S(2)}) collective-permute-start(bf16[264,256]{1,0:T(8,128)(2,1)} %get-tuple-element.63), channel_id=1, source_target_pairs={{0,2},{2,0},{4,6},{6,4},{8,10},{10,8},{12,14},{14,12},{16,18},{18,... | collective-permute-start | bytes 405512 | tf_op jit(solution)/shard_map/ppermute | solution.py:379
  18.6 3.0 %collective-permute-done.13.refs_7_ = bf16[264,256]{1,0:T(8,128)(2,1)S(1)} collective-permute-done((bf16[264,256]{1,0:T(8,128)(2,1)}, bf16[264,256]{1,0:T(8,128)(2,1)S(1)}, u32[]{:S(2)}, u32[]{:S(2)}) %collective-permute-start.13) | collective-permute-done | bytes 135200 | tf_op jit(solution)/shard_map/ppermute | solution.py:379
  21.6 4.0 %collective-permute-done.8.refs_2_ = bf16[264,256]{1,0:T(8,128)(2,1)S(1)} collective-permute-done((bf16[264,256]{1,0:T(8,128)(2,1)}, bf16[264,256]{1,0:T(8,128)(2,1)S(1)}, u32[]{:S(2)}, u32[]{:S(2)}) %collective-permute-start.8) | collective-permute-done | bytes 135200 | tf_op jit(solution)/shard_map/ppermute | solution.py:379
  27.5 2.6 %collective-permute-start.14 = (bf16[8,128,256]{2,1,0:T(8,128)(2,1)S(1)}, bf16[8,128,256]{2,1,0:T(8,128)(2,1)S(1)}, u32[]{:S(2)}, u32[]{:S(2)}) collective-permute-start(bf16[8,128,256]{2,1,0:T(8,128)(2,1)S(1)} %get-tuple-element.70), channel_id=1, source_target_pairs={{0,16},{2,18},{4,20},{6,22},{8,24},{10,26},{12,28},{14,30},{16,0},... | collective-permute-start | bytes 1572872 | tf_op jit(solution)/shard_map/ppermute | solution.py:379
  37.5 2.2 %collective-permute-start.4 = (bf16[264,256]{1,0:T(8,128)(2,1)S(1)}, bf16[264,256]{1,0:T(8,128)(2,1)S(1)}, u32[]{:S(2)}, u32[]{:S(2)}) collective-permute-start(bf16[264,256]{1,0:T(8,128)(2,1)S(1)} %get-tuple-element.59), channel_id=1, source_target_pairs={{0,10},{2,8},{4,14},{6,12},{8,2},{10,0},{12,6},{14,4},{16,26},{18,... | collective-permute-start | bytes 405512 | tf_op jit(solution)/shard_map/ppermute | solution.py:379
  43.6 1.7 %collective-permute-done.3.refs_4_ = bf16[264,256]{1,0:T(8,128)(2,1)S(1)} collective-permute-done((bf16[264,256]{1,0:T(8,128)(2,1)S(1)}, bf16[264,256]{1,0:T(8,128)(2,1)S(1)}, u32[]{:S(2)}, u32[]{:S(2)}) %collective-permute-start.3) | collective-permute-done | bytes 135200 | tf_op jit(solution)/shard_map/ppermute | solution.py:379
  45.4 9.6 %collective-permute-done.4.refs_5_ = bf16[264,256]{1,0:T(8,128)(2,1)S(1)} collective-permute-done((bf16[264,256]{1,0:T(8,128)(2,1)S(1)}, bf16[264,256]{1,0:T(8,128)(2,1)S(1)}, u32[]{:S(2)}, u32[]{:S(2)}) %collective-permute-start.4) | collective-permute-done | bytes 135200 | tf_op jit(solution)/shard_map/ppermute | solution.py:379
  55.0 2.7 %collective-permute-done.5.refs_6_ = bf16[264,256]{1,0:T(8,128)(2,1)S(1)} collective-permute-done((bf16[264,256]{1,0:T(8,128)(2,1)S(1)}, bf16[264,256]{1,0:T(8,128)(2,1)S(1)}, u32[]{:S(2)}, u32[]{:S(2)}) %collective-permute-start.5) | collective-permute-done | bytes 135200 | tf_op jit(solution)/shard_map/ppermute | solution.py:379
  60.6 1.9 %collective-permute-done.15.refs_1_ = bf16[1024,256]{1,0:T(8,128)(2,1)S(1)} collective-permute-done((bf16[1024,256]{1,0:T(8,128)(2,1)S(1)}, bf16[1024,256]{1,0:T(8,128)(2,1)S(1)}, u32[]{:S(2)}, u32[]{:S(2)}) %collective-permute-start.15) | collective-permute-done | bytes 524320 | tf_op jit(solution)/shard_map/ppermute | solution.py:391
  63.8 1.8 %collective-permute-done.16.refs_1_.refs_5_ = bf16[1024,256]{1,0:T(8,128)(2,1)S(1)} collective-permute-done((bf16[1024,256]{1,0:T(8,128)(2,1)S(1)}, bf16[1024,256]{1,0:T(8,128)(2,1)S(1)}, u32[]{:S(2)}, u32[]{:S(2)}) %collective-permute-start.16) | collective-permute-done | bytes 524320 | tf_op jit(solution)/shard_map/ppermute | solution.py:391
  71.4 5.7 %collective-permute-done.17.refs_3_.refs_7_ = bf16[512,256]{1,0:T(8,128)(2,1)S(1)} collective-permute-done((bf16[512,256]{1,0:T(8,128)(2,1)S(1)}, bf16[512,256]{1,0:T(8,128)(2,1)S(1)}, u32[]{:S(2)}, u32[]{:S(2)}) %collective-permute-start.17) | collective-permute-done | bytes 262176 | tf_op jit(solution)/shard_map/ppermute | solution.py:379
  77.1 5.8 %collective-permute-done.18.refs_4_.refs_8_ = bf16[512,256]{1,0:T(8,128)(2,1)S(1)} collective-permute-done((bf16[512,256]{1,0:T(8,128)(2,1)S(1)}, bf16[512,256]{1,0:T(8,128)(2,1)S(1)}, u32[]{:S(2)}, u32[]{:S(2)}) %collective-permute-start.18) | collective-permute-done | bytes 262176 | tf_op jit(solution)/shard_map/ppermute | solution.py:379
  83.6 2.2 %collective-permute-start.26 = (bf16[256,256]{1,0:T(8,128)(2,1)S(1)}, bf16[256,256]{1,0:T(8,128)(2,1)S(1)}, u32[]{:S(2)}, u32[]{:S(2)}) collective-permute-start(bf16[256,256]{1,0:T(8,128)(2,1)S(1)} %get-tuple-element.87), channel_id=1, source_target_pairs={{0,10},{2,8},{4,14},{6,12},{8,2},{10,0},{12,6},{14,4},{16,26},{18,... | collective-permute-start | bytes 393224 | tf_op jit(solution)/shard_map/ppermute | solution.py:379
  86.3 3.1 %collective-permute-start.28 = (bf16[256,256]{1,0:T(8,128)(2,1)S(1)}, bf16[256,256]{1,0:T(8,128)(2,1)S(1)}, u32[]{:S(2)}, u32[]{:S(2)}) collective-permute-start(bf16[256,256]{1,0:T(8,128)(2,1)S(1)} %get-tuple-element.89), channel_id=1, source_target_pairs={{0,14},{2,12},{4,10},{6,8},{8,6},{10,4},{12,2},{14,0},{16,30},{18,... | collective-permute-start | bytes 393224 | tf_op jit(solution)/shard_map/ppermute | solution.py:379
  89.5 12.0 %collective-permute-done.20.holder.refs_10_ = bf16[512,256]{1,0:T(8,128)(2,1)S(1)} collective-permute-done((bf16[512,256]{1,0:T(8,128)(2,1)S(1)}, bf16[512,256]{1,0:T(8,128)(2,1)S(1)}, u32[]{:S(2)}, u32[]{:S(2)}) %collective-permute-start.20) | collective-permute-done | bytes 262176 | tf_op jit(solution)/shard_map/ppermute | solution.py:379
  108.8 4.9 %collective-permute-done.28.refs_13_ = bf16[256,256]{1,0:T(8,128)(2,1)S(1)} collective-permute-done((bf16[256,256]{1,0:T(8,128)(2,1)S(1)}, bf16[256,256]{1,0:T(8,128)(2,1)S(1)}, u32[]{:S(2)}, u32[]{:S(2)}) %collective-permute-start.28) | collective-permute-done | bytes 131104 | tf_op jit(solution)/shard_map/ppermute | solution.py:379
  113.7 2.2 %collective-permute-start.33 = (bf16[256,256]{1,0:T(8,128)(2,1)S(1)}, bf16[256,256]{1,0:T(8,128)(2,1)S(1)}, u32[]{:S(2)}, u32[]{:S(2)}) collective-permute-start(bf16[256,256]{1,0:T(8,128)(2,1)S(1)} %get-tuple-element.95), channel_id=1, source_target_pairs={{0,10},{2,8},{4,14},{6,12},{8,2},{10,0},{12,6},{14,4},{16,26},{18,... | collective-permute-start | bytes 393224 | tf_op jit(solution)/shard_map/ppermute | solution.py:379
  116.7 3.0 %collective-permute-start.35 = (bf16[256,256]{1,0:T(8,128)(2,1)S(1)}, bf16[256,256]{1,0:T(8,128)(2,1)S(1)}, u32[]{:S(2)}, u32[]{:S(2)}) collective-permute-start(bf16[256,256]{1,0:T(8,128)(2,1)S(1)} %get-tuple-element.97), channel_id=1, source_target_pairs={{0,14},{2,12},{4,10},{6,8},{8,6},{10,4},{12,2},{14,0},{16,30},{18,... | collective-permute-start | bytes 393224 | tf_op jit(solution)/shard_map/ppermute | solution.py:379
  125.9 2.6 %collective-permute-done.35.refs_20_ = bf16[256,256]{1,0:T(8,128)(2,1)S(1)} collective-permute-done((bf16[256,256]{1,0:T(8,128)(2,1)S(1)}, bf16[256,256]{1,0:T(8,128)(2,1)S(1)}, u32[]{:S(2)}, u32[]{:S(2)}) %collective-permute-start.35) | collective-permute-done | bytes 131104 | tf_op jit(solution)/shard_map/ppermute | solution.py:379
  128.4 2.2 %shard_map.162 = bf16[8,128,256]{2,1,0:T(8,128)(2,1)} custom-call(s32[16]{0:T(128)S(1)} %copy-done.12, s32[16]{0:T(128)S(1)} %copy-done.13, s32[32]{0:T(128)S(1)} %copy-done.9, bf16[16,128,128]{2,1,0:T(8,128)(2,1)S(1)} %copy-done.1, bf16[8,128,256]{2,1,0:T(8,128)(2,1)S(1)} %shard_map.154.refs_1_.back.refs_4_, ...), custom_call_target="tpu_custom_call" | custom-call | flops 1048576 | bytes 1048576 | tf_op jit(solution)/shard_map/pallas_call | solution.py:29
  130.6 1.8 %collective-permute-done.23.refs_2_ = bf16[128,512]{1,0:T(8,128)(2,1)S(1)} collective-permute-done((bf16[128,512]{1,0:T(8,128)(2,1)S(1)}, bf16[128,512]{1,0:T(8,128)(2,1)S(1)}, u32[]{:S(2)}, u32[]{:S(2)}) %collective-permute-start.23) | collective-permute-done | bytes 131104 | tf_op jit(solution)/shard_map/ppermute | solution.py:379
  (94 shorter events, 47.0 us)
Async XLA Ops:
  8.4 10.3 %collective-permute-start.12 = (bf16[264,256]{1,0:T(8,128)(2,1)}, bf16[264,256]{1,0:T(8,128)(2,1)S(1)}, u32[]{:S(2)}, u32[]{:S(2)}) collective-permute-start(bf16[264,256]{1,0:T(8,128)(2,1)} %get-tuple-element.68), channel_id=1, source_target_pairs={{0,12},{2,14},{4,8},{6,10},{8,4},{10,6},{12,0},{14,2},{16,28},{18,... | collective-permute-start | bytes 405512 | tf_op jit(solution)/shard_map/ppermute | solution.py:379
  10.9 10.7 %collective-permute-start.13 = (bf16[264,256]{1,0:T(8,128)(2,1)}, bf16[264,256]{1,0:T(8,128)(2,1)S(1)}, u32[]{:S(2)}, u32[]{:S(2)}) collective-permute-start(bf16[264,256]{1,0:T(8,128)(2,1)} %get-tuple-element.69), channel_id=1, source_target_pairs={{0,14},{2,12},{4,10},{6,8},{8,6},{10,4},{12,2},{14,0},{16,30},{18,... | collective-permute-start | bytes 405512 | tf_op jit(solution)/shard_map/ppermute | solution.py:379
  10.9 10.7 %collective-permute-start.7 = (bf16[264,256]{1,0:T(8,128)(2,1)}, bf16[264,256]{1,0:T(8,128)(2,1)S(1)}, u32[]{:S(2)}, u32[]{:S(2)}) collective-permute-start(bf16[264,256]{1,0:T(8,128)(2,1)} %get-tuple-element.63), channel_id=1, source_target_pairs={{0,2},{2,0},{4,6},{6,4},{8,10},{10,8},{12,14},{14,12},{16,18},{18,... | collective-permute-start | bytes 405512 | tf_op jit(solution)/shard_map/ppermute | solution.py:379
  12.8 12.8 %collective-permute-start.8 = (bf16[264,256]{1,0:T(8,128)(2,1)}, bf16[264,256]{1,0:T(8,128)(2,1)S(1)}, u32[]{:S(2)}, u32[]{:S(2)}) collective-permute-start(bf16[264,256]{1,0:T(8,128)(2,1)} %get-tuple-element.64), channel_id=1, source_target_pairs={{0,4},{2,6},{4,0},{6,2},{8,12},{10,14},{12,8},{14,10},{16,20},{18,... | collective-permute-start | bytes 405512 | tf_op jit(solution)/shard_map/ppermute | solution.py:379
  27.5 31.6 %collective-permute-start.14 = (bf16[8,128,256]{2,1,0:T(8,128)(2,1)S(1)}, bf16[8,128,256]{2,1,0:T(8,128)(2,1)S(1)}, u32[]{:S(2)}, u32[]{:S(2)}) collective-permute-start(bf16[8,128,256]{2,1,0:T(8,128)(2,1)S(1)} %get-tuple-element.70), channel_id=1, source_target_pairs={{0,16},{2,18},{4,20},{6,22},{8,24},{10,26},{12,28},{14,30},{16,0},... | collective-permute-start | bytes 1572872 | tf_op jit(solution)/shard_map/ppermute | solution.py:379
  35.1 10.2 %collective-permute-start.3 = (bf16[264,256]{1,0:T(8,128)(2,1)S(1)}, bf16[264,256]{1,0:T(8,128)(2,1)S(1)}, u32[]{:S(2)}, u32[]{:S(2)}) collective-permute-start(bf16[264,256]{1,0:T(8,128)(2,1)S(1)} %get-tuple-element.58), channel_id=1, source_target_pairs={{0,8},{2,10},{4,12},{6,14},{8,0},{10,2},{12,4},{14,6},{16,24},{18,... | collective-permute-start | bytes 405512 | tf_op jit(solution)/shard_map/ppermute | solution.py:379
  37.5 17.5 %collective-permute-start.4 = (bf16[264,256]{1,0:T(8,128)(2,1)S(1)}, bf16[264,256]{1,0:T(8,128)(2,1)S(1)}, u32[]{:S(2)}, u32[]{:S(2)}) collective-permute-start(bf16[264,256]{1,0:T(8,128)(2,1)S(1)} %get-tuple-element.59), channel_id=1, source_target_pairs={{0,10},{2,8},{4,14},{6,12},{8,2},{10,0},{12,6},{14,4},{16,26},{18,... | collective-permute-start | bytes 405512 | tf_op jit(solution)/shard_map/ppermute | solution.py:379
  39.7 18.0 %collective-permute-start.5 = (bf16[264,256]{1,0:T(8,128)(2,1)S(1)}, bf16[264,256]{1,0:T(8,128)(2,1)S(1)}, u32[]{:S(2)}, u32[]{:S(2)}) collective-permute-start(bf16[264,256]{1,0:T(8,128)(2,1)S(1)} %get-tuple-element.60), channel_id=1, source_target_pairs={{0,12},{2,14},{4,8},{6,10},{8,4},{10,6},{12,0},{14,2},{16,28},{18,... | collective-permute-start | bytes 405512 | tf_op jit(solution)/shard_map/ppermute | solution.py:379
  41.4 17.8 %collective-permute-start.6 = (bf16[264,256]{1,0:T(8,128)(2,1)S(1)}, bf16[264,256]{1,0:T(8,128)(2,1)S(1)}, u32[]{:S(2)}, u32[]{:S(2)}) collective-permute-start(bf16[264,256]{1,0:T(8,128)(2,1)S(1)} %get-tuple-element.61), channel_id=1, source_target_pairs={{0,14},{2,12},{4,10},{6,8},{8,6},{10,4},{12,2},{14,0},{16,30},{18,... | collective-permute-start | bytes 405512 | tf_op jit(solution)/shard_map/ppermute | solution.py:379
  69.2 13.7 %collective-permute-start.18 = (bf16[512,256]{1,0:T(8,128)(2,1)S(1)}, bf16[512,256]{1,0:T(8,128)(2,1)S(1)}, u32[]{:S(2)}, u32[]{:S(2)}) collective-permute-start(bf16[512,256]{1,0:T(8,128)(2,1)S(1)} %get-tuple-element.81), channel_id=1, source_target_pairs={{0,4},{2,6},{4,0},{6,2},{8,12},{10,14},{12,8},{14,10},{16,20},{18,... | collective-permute-start | bytes 786440 | tf_op jit(solution)/shard_map/ppermute | solution.py:379
  70.0 12.9 %collective-permute-start.19 = (bf16[512,256]{1,0:T(8,128)(2,1)S(1)}, bf16[512,256]{1,0:T(8,128)(2,1)S(1)}, u32[]{:S(2)}, u32[]{:S(2)}) collective-permute-start(bf16[512,256]{1,0:T(8,128)(2,1)S(1)} %get-tuple-element.82), channel_id=1, source_target_pairs={{0,6},{2,4},{4,2},{6,0},{8,14},{10,12},{12,10},{14,8},{16,22},{18,... | collective-permute-start | bytes 786440 | tf_op jit(solution)/shard_map/ppermute | solution.py:379
  71.4 30.3 %collective-permute-start.25 = (bf16[8,128,256]{2,1,0:T(8,128)(2,1)S(1)}, bf16[8,128,256]{2,1,0:T(8,128)(2,1)S(1)}, u32[]{:S(2)}, u32[]{:S(2)}) collective-permute-start(bf16[8,128,256]{2,1,0:T(8,128)(2,1)S(1)} %shard_map.154.refs_1_.back.refs_4_), channel_id=1, source_target_pairs={{0,16},{2,18},{4,20},{6,22},{8,24},{10,26},{12,28},{14,30},{16,0},... | collective-permute-start | bytes 1572872 | tf_op jit(solution)/shard_map/ppermute | solution.py:379
  83.5 18.0 %collective-permute-start.20 = (bf16[512,256]{1,0:T(8,128)(2,1)S(1)}, bf16[512,256]{1,0:T(8,128)(2,1)S(1)}, u32[]{:S(2)}, u32[]{:S(2)}) collective-permute-start(bf16[512,256]{1,0:T(8,128)(2,1)S(1)} %get-tuple-element.84), channel_id=1, source_target_pairs={{0,8},{2,10},{4,12},{6,14},{8,0},{10,2},{12,4},{14,6},{16,24},{18,... | collective-permute-start | bytes 786440 | tf_op jit(solution)/shard_map/ppermute | solution.py:379
  83.6 20.8 %collective-permute-start.26 = (bf16[256,256]{1,0:T(8,128)(2,1)S(1)}, bf16[256,256]{1,0:T(8,128)(2,1)S(1)}, u32[]{:S(2)}, u32[]{:S(2)}) collective-permute-start(bf16[256,256]{1,0:T(8,128)(2,1)S(1)} %get-tuple-element.87), channel_id=1, source_target_pairs={{0,10},{2,8},{4,14},{6,12},{8,2},{10,0},{12,6},{14,4},{16,26},{18,... | collective-permute-start | bytes 393224 | tf_op jit(solution)/shard_map/ppermute | solution.py:379
  85.8 21.6 %collective-permute-start.27 = (bf16[256,256]{1,0:T(8,128)(2,1)S(1)}, bf16[256,256]{1,0:T(8,128)(2,1)S(1)}, u32[]{:S(2)}, u32[]{:S(2)}) collective-permute-start(bf16[256,256]{1,0:T(8,128)(2,1)S(1)} %get-tuple-element.88), channel_id=1, source_target_pairs={{0,12},{2,14},{4,8},{6,10},{8,4},{10,6},{12,0},{14,2},{16,28},{18,... | collective-permute-start | bytes 393224 | tf_op jit(solution)/shard_map/ppermute | solution.py:379
  86.3 27.3 %collective-permute-start.28 = (bf16[256,256]{1,0:T(8,128)(2,1)S(1)}, bf16[256,256]{1,0:T(8,128)(2,1)S(1)}, u32[]{:S(2)}, u32[]{:S(2)}) collective-permute-start(bf16[256,256]{1,0:T(8,128)(2,1)S(1)} %get-tuple-element.89), channel_id=1, source_target_pairs={{0,14},{2,12},{4,10},{6,8},{8,6},{10,4},{12,2},{14,0},{16,30},{18,... | collective-permute-start | bytes 393224 | tf_op jit(solution)/shard_map/ppermute | solution.py:379
  101.5 12.1 %collective-permute-start.21 = (bf16[128,512]{1,0:T(8,128)(2,1)S(1)}, bf16[128,512]{1,0:T(8,128)(2,1)S(1)}, u32[]{:S(2)}, u32[]{:S(2)}) collective-permute-start(bf16[128,512]{1,0:T(8,128)(2,1)S(1)} %shard_map.157.total), channel_id=1, source_target_pairs={{0,16},{2,18},{4,20},{6,22},{8,24},{10,26},{12,28},{14,30},{16,0},... | collective-permute-start | bytes 393224 | tf_op jit(solution)/shard_map/ppermute | solution.py:379
  102.4 13.4 %collective-permute-start.29 = (bf16[256,256]{1,0:T(8,128)(2,1)S(1)}, bf16[256,256]{1,0:T(8,128)(2,1)S(1)}, u32[]{:S(2)}, u32[]{:S(2)}) collective-permute-start(bf16[256,256]{1,0:T(8,128)(2,1)S(1)} %get-tuple-element.91), channel_id=1, source_target_pairs={{0,2},{2,0},{4,6},{6,4},{8,10},{10,8},{12,14},{14,12},{16,18},{18,... | collective-permute-start | bytes 393224 | tf_op jit(solution)/shard_map/ppermute | solution.py:379
  104.4 12.3 %collective-permute-start.30 = (bf16[256,256]{1,0:T(8,128)(2,1)S(1)}, bf16[256,256]{1,0:T(8,128)(2,1)S(1)}, u32[]{:S(2)}, u32[]{:S(2)}) collective-permute-start(bf16[256,256]{1,0:T(8,128)(2,1)S(1)} %get-tuple-element.92), channel_id=1, source_target_pairs={{0,4},{2,6},{4,0},{6,2},{8,12},{10,14},{12,8},{14,10},{16,20},{18,... | collective-permute-start | bytes 393224 | tf_op jit(solution)/shard_map/ppermute | solution.py:379
  107.5 12.2 %collective-permute-start.31 = (bf16[256,256]{1,0:T(8,128)(2,1)S(1)}, bf16[256,256]{1,0:T(8,128)(2,1)S(1)}, u32[]{:S(2)}, u32[]{:S(2)}) collective-permute-start(bf16[256,256]{1,0:T(8,128)(2,1)S(1)} %get-tuple-element.93), channel_id=1, source_target_pairs={{0,6},{2,4},{4,2},{6,0},{8,14},{10,12},{12,10},{14,8},{16,22},{18,... | collective-permute-start | bytes 393224 | tf_op jit(solution)/shard_map/ppermute | solution.py:379
  115.9 10.0 %collective-permute-start.34 = (bf16[256,256]{1,0:T(8,128)(2,1)S(1)}, bf16[256,256]{1,0:T(8,128)(2,1)S(1)}, u32[]{:S(2)}, u32[]{:S(2)}) collective-permute-start(bf16[256,256]{1,0:T(8,128)(2,1)S(1)} %get-tuple-element.96), channel_id=1, source_target_pairs={{0,12},{2,14},{4,8},{6,10},{8,4},{10,6},{12,0},{14,2},{16,28},{18,... | collective-permute-start | bytes 393224 | tf_op jit(solution)/shard_map/ppermute | solution.py:379
  116.7 11.7 %collective-permute-start.35 = (bf16[256,256]{1,0:T(8,128)(2,1)S(1)}, bf16[256,256]{1,0:T(8,128)(2,1)S(1)}, u32[]{:S(2)}, u32[]{:S(2)}) collective-permute-start(bf16[256,256]{1,0:T(8,128)(2,1)S(1)} %get-tuple-element.97), channel_id=1, source_target_pairs={{0,14},{2,12},{4,10},{6,8},{8,6},{10,4},{12,2},{14,0},{16,30},{18,... | collective-permute-start | bytes 393224 | tf_op jit(solution)/shard_map/ppermute | solution.py:379
  119.7 10.9 %collective-permute-start.22 = (bf16[128,512]{1,0:T(8,128)(2,1)S(1)}, bf16[128,512]{1,0:T(8,128)(2,1)S(1)}, u32[]{:S(2)}, u32[]{:S(2)}) collective-permute-start(bf16[128,512]{1,0:T(8,128)(2,1)S(1)} %shard_map.158.refs_0_), channel_id=1, source_target_pairs={{0,2},{2,0},{4,6},{6,4},{8,10},{10,8},{12,14},{14,12},{16,18},{18,... | collective-permute-start | bytes 393224 | tf_op jit(solution)/shard_map/ppermute | solution.py:379
  120.4 12.0 %collective-permute-start.23 = (bf16[128,512]{1,0:T(8,128)(2,1)S(1)}, bf16[128,512]{1,0:T(8,128)(2,1)S(1)}, u32[]{:S(2)}, u32[]{:S(2)}) collective-permute-start(bf16[128,512]{1,0:T(8,128)(2,1)S(1)} %shard_map.158.refs_0_), channel_id=1, source_target_pairs={{0,4},{2,6},{4,0},{6,2},{8,12},{10,14},{12,8},{14,10},{16,20},{18,... | collective-permute-start | bytes 393224 | tf_op jit(solution)/shard_map/ppermute | solution.py:379
  (27 other events, 219.3 us)

commit v2 on v0

--- a/solution.py
+++ b/solution.py
@@ -342,9 +342,13 @@
     return lax.ppermute(value, "dom", pairs)
 
 
+def nearest_first(top, bottom=1):
+    return sorted(range(bottom, top), key=lambda k: (k.bit_count(), -k))
+
+
 def swap_all(values, first):
     out = [values[0]] + [None] * (len(values) - 1)
-    for k in range(len(values) - 1, 0, -1):
+    for k in nearest_first(len(values)):
         out[k] = swap(values[k], k * first)
     return out
 
@@ -424,7 +428,7 @@
     )
     crossed = swap(dense, half)
     near_late = [None] * (half - early)
-    for k in range(half - 1, early - 1, -1):
+    for k in nearest_first(half, early):
         near_late[k - early] = swap(near[k], k)
     direct = near_early + near_late
 

time: 128 us -> 128 us (level)
  no operation moved by 1% of the time
where the time goes in v2:
time: 128 us
  waiting for transfers between devices  63.4 us (50%)
  starting transfers between devices  45.8 us (36%)
  Pallas kernels  16.4 us (13%)
  local copies, waits for them, and re-layouts  1.64 us (1%)
    ppermute x38, waiting for transfers between devices, swap(): return lax.ppermute(value, 'dom', pairs)  59.7 us
    ppermute x38, starting transfers between devices, swap(): return lax.ppermute(value, 'dom', pairs)  45.6 us
    pallas_call x17, Pallas kernels, call(): pl.pallas_call(kernel, out_shape=tuple((out for _, out in outs)), in_spec...  16.4 us
    ppermute x2, waiting for transfers between devices, around(): lax.ppermute(value, 'chan', [(at, (at + shift) % count) for at in range(c...  3.67 us
  transfers between devices with their start and end apart: 40, of which 28 were waited for; matrix products, arithmetic and copies ran while one was open for 0% of the time, Pallas kernels for 5%

profile of v2, /device:TPU:0, one launch (start us, length us, event | category | flops | bytes accessed | tf_op | source)
XLA Modules:
  0.0 128.1 jit_solution(16216709392532571095)
XLA Ops:
  0.6 3.3 %shard_map.147 = (bf16[264,256]{1,0:T(8,128)(2,1)}, bf16[264,256]{1,0:T(8,128)(2,1)}, bf16[264,256]{1,0:T(8,128)(2,1)}, bf16[264,256]{1,0:T(8,128)(2,1)}, bf16[2...) custom-call(s32[16]{0:T(128)} %refs_0_.5, ...), custom_call_target="tpu_custom_call" | custom-call | flops 1048576 | bytes 1048576 | tf_op jit(solution)/shard_map/pallas_call | solution.py:29
  3.9 3.0 %collective-permute-start.7 = (bf16[264,256]{1,0:T(8,128)(2,1)}, bf16[264,256]{1,0:T(8,128)(2,1)S(1)}, u32[]{:S(2)}, u32[]{:S(2)}) collective-permute-start(bf16[264,256]{1,0:T(8,128)(2,1)} %get-tuple-element.65), channel_id=1, source_target_pairs={{0,2},{2,0},{4,6},{6,4},{8,10},{10,8},{12,14},{14,12},{16,18},{18,... | collective-permute-start | bytes 405512 | tf_op jit(solution)/shard_map/ppermute | solution.py:342
  8.5 2.0 %collective-permute-start.10 = (bf16[264,256]{1,0:T(8,128)(2,1)}, bf16[264,256]{1,0:T(8,128)(2,1)S(1)}, u32[]{:S(2)}, u32[]{:S(2)}) collective-permute-start(bf16[264,256]{1,0:T(8,128)(2,1)} %get-tuple-element.68), channel_id=1, source_target_pairs={{0,8},{2,10},{4,12},{6,14},{8,0},{10,2},{12,4},{14,6},{16,24},{18,... | collective-permute-start | bytes 405512 | tf_op jit(solution)/shard_map/ppermute | solution.py:342
  11.9 2.5 %collective-permute-start.12 = (bf16[264,256]{1,0:T(8,128)(2,1)}, bf16[264,256]{1,0:T(8,128)(2,1)S(1)}, u32[]{:S(2)}, u32[]{:S(2)}) collective-permute-start(bf16[264,256]{1,0:T(8,128)(2,1)} %get-tuple-element.70), channel_id=1, source_target_pairs={{0,12},{2,14},{4,8},{6,10},{8,4},{10,6},{12,0},{14,2},{16,28},{18,... | collective-permute-start | bytes 405512 | tf_op jit(solution)/shard_map/ppermute | solution.py:342
  16.2 3.2 %collective-permute-done.11.refs_5_ = bf16[264,256]{1,0:T(8,128)(2,1)S(1)} collective-permute-done((bf16[264,256]{1,0:T(8,128)(2,1)}, bf16[264,256]{1,0:T(8,128)(2,1)S(1)}, u32[]{:S(2)}, u32[]{:S(2)}) %collective-permute-start.11) | collective-permute-done | bytes 135200 | tf_op jit(solution)/shard_map/ppermute | solution.py:342
  19.4 2.9 %collective-permute-done.12.refs_6_ = bf16[264,256]{1,0:T(8,128)(2,1)S(1)} collective-permute-done((bf16[264,256]{1,0:T(8,128)(2,1)}, bf16[264,256]{1,0:T(8,128)(2,1)S(1)}, u32[]{:S(2)}, u32[]{:S(2)}) %collective-permute-start.12) | collective-permute-done | bytes 135200 | tf_op jit(solution)/shard_map/ppermute | solution.py:342
  22.3 1.9 %collective-permute-done.13.refs_7_ = bf16[264,256]{1,0:T(8,128)(2,1)S(1)} collective-permute-done((bf16[264,256]{1,0:T(8,128)(2,1)}, bf16[264,256]{1,0:T(8,128)(2,1)S(1)}, u32[]{:S(2)}, u32[]{:S(2)}) %collective-permute-start.13) | collective-permute-done | bytes 135200 | tf_op jit(solution)/shard_map/ppermute | solution.py:342
  26.1 2.6 %collective-permute-start.14 = (bf16[8,128,256]{2,1,0:T(8,128)(2,1)S(1)}, bf16[8,128,256]{2,1,0:T(8,128)(2,1)S(1)}, u32[]{:S(2)}, u32[]{:S(2)}) collective-permute-start(bf16[8,128,256]{2,1,0:T(8,128)(2,1)S(1)} %get-tuple-element.72), channel_id=1, source_target_pairs={{0,16},{2,18},{4,20},{6,22},{8,24},{10,26},{12,28},{14,30},{16,0},... | collective-permute-start | bytes 1572872 | tf_op jit(solution)/shard_map/ppermute | solution.py:342
  32.0 1.8 %collective-permute-start.2 = (bf16[264,256]{1,0:T(8,128)(2,1)S(1)}, bf16[264,256]{1,0:T(8,128)(2,1)S(1)}, u32[]{:S(2)}, u32[]{:S(2)}) collective-permute-start(bf16[264,256]{1,0:T(8,128)(2,1)S(1)} %get-tuple-element.59), channel_id=1, source_target_pairs={{0,6},{2,4},{4,2},{6,0},{8,14},{10,12},{12,10},{14,8},{16,22},{18,... | collective-permute-start | bytes 405512 | tf_op jit(solution)/shard_map/ppermute | solution.py:342
  35.3 2.0 %collective-permute-done.refs_1_ = bf16[264,256]{1,0:T(8,128)(2,1)S(1)} collective-permute-done((bf16[264,256]{1,0:T(8,128)(2,1)S(1)}, bf16[264,256]{1,0:T(8,128)(2,1)S(1)}, u32[]{:S(2)}, u32[]{:S(2)}) %collective-permute-start) | collective-permute-done | bytes 135200 | tf_op jit(solution)/shard_map/ppermute | solution.py:342
  41.7 8.5 %collective-permute-done.3.refs_4_ = bf16[264,256]{1,0:T(8,128)(2,1)S(1)} collective-permute-done((bf16[264,256]{1,0:T(8,128)(2,1)S(1)}, bf16[264,256]{1,0:T(8,128)(2,1)S(1)}, u32[]{:S(2)}, u32[]{:S(2)}) %collective-permute-start.3) | collective-permute-done | bytes 135200 | tf_op jit(solution)/shard_map/ppermute | solution.py:342
  50.2 4.1 %collective-permute-done.4.refs_5_ = bf16[264,256]{1,0:T(8,128)(2,1)S(1)} collective-permute-done((bf16[264,256]{1,0:T(8,128)(2,1)S(1)}, bf16[264,256]{1,0:T(8,128)(2,1)S(1)}, u32[]{:S(2)}, u32[]{:S(2)}) %collective-permute-start.4) | collective-permute-done | bytes 135200 | tf_op jit(solution)/shard_map/ppermute | solution.py:342
  55.2 2.1 %collective-permute-done.6.refs_7_ = bf16[264,256]{1,0:T(8,128)(2,1)S(1)} collective-permute-done((bf16[264,256]{1,0:T(8,128)(2,1)S(1)}, bf16[264,256]{1,0:T(8,128)(2,1)S(1)}, u32[]{:S(2)}, u32[]{:S(2)}) %collective-permute-start.6) | collective-permute-done | bytes 135200 | tf_op jit(solution)/shard_map/ppermute | solution.py:342
  58.8 1.9 %collective-permute-done.15.refs_1_ = bf16[1024,256]{1,0:T(8,128)(2,1)S(1)} collective-permute-done((bf16[1024,256]{1,0:T(8,128)(2,1)S(1)}, bf16[1024,256]{1,0:T(8,128)(2,1)S(1)}, u32[]{:S(2)}, u32[]{:S(2)}) %collective-permute-start.15) | collective-permute-done | bytes 524320 | tf_op jit(solution)/shard_map/ppermute | solution.py:358
  62.0 1.8 %collective-permute-done.16.refs_3_.refs_1_ = bf16[1024,256]{1,0:T(8,128)(2,1)S(1)} collective-permute-done((bf16[1024,256]{1,0:T(8,128)(2,1)S(1)}, bf16[1024,256]{1,0:T(8,128)(2,1)S(1)}, u32[]{:S(2)}, u32[]{:S(2)}) %collective-permute-start.16) | collective-permute-done | bytes 524320 | tf_op jit(solution)/shard_map/ppermute | solution.py:358
  70.6 1.8 %collective-permute-done.18.refs_2_ = bf16[128,512]{1,0:T(8,128)(2,1)S(1)} collective-permute-done((bf16[128,512]{1,0:T(8,128)(2,1)S(1)}, bf16[128,512]{1,0:T(8,128)(2,1)S(1)}, u32[]{:S(2)}, u32[]{:S(2)}) %collective-permute-start.18) | collective-permute-done | bytes 131104 | tf_op jit(solution)/shard_map/ppermute | solution.py:342
  79.4 2.3 %collective-permute-done.20.refs_1_ = bf16[128,512]{1,0:T(8,128)(2,1)S(1)} collective-permute-done((bf16[128,512]{1,0:T(8,128)(2,1)S(1)}, bf16[128,512]{1,0:T(8,128)(2,1)S(1)}, u32[]{:S(2)}, u32[]{:S(2)}) %collective-permute-start.20) | collective-permute-done | bytes 131104 | tf_op jit(solution)/shard_map/ppermute | solution.py:342
  81.8 2.0 %collective-permute-start.21 = (bf16[128,512]{1,0:T(8,128)(2,1)S(1)}, bf16[128,512]{1,0:T(8,128)(2,1)S(1)}, u32[]{:S(2)}, u32[]{:S(2)}) collective-permute-start(bf16[128,512]{1,0:T(8,128)(2,1)S(1)} %shard_map.156.refs_0_), channel_id=1, source_target_pairs={{0,16},{2,18},{4,20},{6,22},{8,24},{10,26},{12,28},{14,30},{16,0},... | collective-permute-start | bytes 393224 | tf_op jit(solution)/shard_map/ppermute | solution.py:342
  87.3 9.9 %collective-permute-done.21.refs_1_ = bf16[128,512]{1,0:T(8,128)(2,1)S(1)} collective-permute-done((bf16[128,512]{1,0:T(8,128)(2,1)S(1)}, bf16[128,512]{1,0:T(8,128)(2,1)S(1)}, u32[]{:S(2)}, u32[]{:S(2)}) %collective-permute-start.21) | collective-permute-done | bytes 131104 | tf_op jit(solution)/shard_map/ppermute | solution.py:342
  102.4 3.6 %collective-permute-done.31.refs_12_ = bf16[256,256]{1,0:T(8,128)(2,1)S(1)} collective-permute-done((bf16[256,256]{1,0:T(8,128)(2,1)S(1)}, bf16[256,256]{1,0:T(8,128)(2,1)S(1)}, u32[]{:S(2)}, u32[]{:S(2)}) %collective-permute-start.31) | collective-permute-done | bytes 131104 | tf_op jit(solution)/shard_map/ppermute | solution.py:342
  114.9 1.8 %collective-permute-done.34.refs_15_ = bf16[256,256]{1,0:T(8,128)(2,1)S(1)} collective-permute-done((bf16[256,256]{1,0:T(8,128)(2,1)S(1)}, bf16[256,256]{1,0:T(8,128)(2,1)S(1)}, u32[]{:S(2)}, u32[]{:S(2)}) %collective-permute-start.34) | collective-permute-done | bytes 131104 | tf_op jit(solution)/shard_map/ppermute | solution.py:342
  121.1 2.9 %collective-permute-done.38.refs_19_ = bf16[256,256]{1,0:T(8,128)(2,1)S(1)} collective-permute-done((bf16[256,256]{1,0:T(8,128)(2,1)S(1)}, bf16[256,256]{1,0:T(8,128)(2,1)S(1)}, u32[]{:S(2)}, u32[]{:S(2)}) %collective-permute-start.38) | collective-permute-done | bytes 131104 | tf_op jit(solution)/shard_map/ppermute | solution.py:342
  124.0 1.9 %collective-permute-done.39.refs_20_ = bf16[256,256]{1,0:T(8,128)(2,1)S(1)} collective-permute-done((bf16[256,256]{1,0:T(8,128)(2,1)S(1)}, bf16[256,256]{1,0:T(8,128)(2,1)S(1)}, u32[]{:S(2)}, u32[]{:S(2)}) %collective-permute-start.39) | collective-permute-done | bytes 131104 | tf_op jit(solution)/shard_map/ppermute | solution.py:342
  126.0 2.2 %shard_map.163 = bf16[8,128,256]{2,1,0:T(8,128)(2,1)} custom-call(s32[16]{0:T(128)S(1)} %copy-done.12, s32[16]{0:T(128)S(1)} %copy-done.13, s32[32]{0:T(128)S(1)} %copy-done.9, bf16[16,128,128]{2,1,0:T(8,128)(2,1)S(1)} %copy-done.1, bf16[8,128,256]{2,1,0:T(8,128)(2,1)S(1)} %shard_map.159.back.rows.refs_4_, ...), custom_call_target="tpu_custom_call" | custom-call | flops 1048576 | bytes 1048576 | tf_op jit(solution)/shard_map/pallas_call | solution.py:29
  (103 shorter events, 55.3 us)
Async XLA Ops:
  10.5 8.9 %collective-permute-start.11 = (bf16[264,256]{1,0:T(8,128)(2,1)}, bf16[264,256]{1,0:T(8,128)(2,1)S(1)}, u32[]{:S(2)}, u32[]{:S(2)}) collective-permute-start(bf16[264,256]{1,0:T(8,128)(2,1)} %get-tuple-element.69), channel_id=1, source_target_pairs={{0,10},{2,8},{4,14},{6,12},{8,2},{10,0},{12,6},{14,4},{16,26},{18,... | collective-permute-start | bytes 405512 | tf_op jit(solution)/shard_map/ppermute | solution.py:342
  11.9 10.4 %collective-permute-start.12 = (bf16[264,256]{1,0:T(8,128)(2,1)}, bf16[264,256]{1,0:T(8,128)(2,1)S(1)}, u32[]{:S(2)}, u32[]{:S(2)}) collective-permute-start(bf16[264,256]{1,0:T(8,128)(2,1)} %get-tuple-element.70), channel_id=1, source_target_pairs={{0,12},{2,14},{4,8},{6,10},{8,4},{10,6},{12,0},{14,2},{16,28},{18,... | collective-permute-start | bytes 405512 | tf_op jit(solution)/shard_map/ppermute | solution.py:342
  14.4 9.8 %collective-permute-start.13 = (bf16[264,256]{1,0:T(8,128)(2,1)}, bf16[264,256]{1,0:T(8,128)(2,1)S(1)}, u32[]{:S(2)}, u32[]{:S(2)}) collective-permute-start(bf16[264,256]{1,0:T(8,128)(2,1)} %get-tuple-element.71), channel_id=1, source_target_pairs={{0,14},{2,12},{4,10},{6,8},{8,6},{10,4},{12,2},{14,0},{16,30},{18,... | collective-permute-start | bytes 405512 | tf_op jit(solution)/shard_map/ppermute | solution.py:342
  26.1 31.2 %collective-permute-start.14 = (bf16[8,128,256]{2,1,0:T(8,128)(2,1)S(1)}, bf16[8,128,256]{2,1,0:T(8,128)(2,1)S(1)}, u32[]{:S(2)}, u32[]{:S(2)}) collective-permute-start(bf16[8,128,256]{2,1,0:T(8,128)(2,1)S(1)} %get-tuple-element.72), channel_id=1, source_target_pairs={{0,16},{2,18},{4,20},{6,22},{8,24},{10,26},{12,28},{14,30},{16,0},... | collective-permute-start | bytes 1572872 | tf_op jit(solution)/shard_map/ppermute | solution.py:342
  33.7 16.5 %collective-permute-start.3 = (bf16[264,256]{1,0:T(8,128)(2,1)S(1)}, bf16[264,256]{1,0:T(8,128)(2,1)S(1)}, u32[]{:S(2)}, u32[]{:S(2)}) collective-permute-start(bf16[264,256]{1,0:T(8,128)(2,1)S(1)} %get-tuple-element.60), channel_id=1, source_target_pairs={{0,8},{2,10},{4,12},{6,14},{8,0},{10,2},{12,4},{14,6},{16,24},{18,... | collective-permute-start | bytes 405512 | tf_op jit(solution)/shard_map/ppermute | solution.py:342
  37.3 17.0 %collective-permute-start.4 = (bf16[264,256]{1,0:T(8,128)(2,1)S(1)}, bf16[264,256]{1,0:T(8,128)(2,1)S(1)}, u32[]{:S(2)}, u32[]{:S(2)}) collective-permute-start(bf16[264,256]{1,0:T(8,128)(2,1)S(1)} %get-tuple-element.61), channel_id=1, source_target_pairs={{0,10},{2,8},{4,14},{6,12},{8,2},{10,0},{12,6},{14,4},{16,26},{18,... | collective-permute-start | bytes 405512 | tf_op jit(solution)/shard_map/ppermute | solution.py:342
  37.4 17.9 %collective-permute-start.5 = (bf16[264,256]{1,0:T(8,128)(2,1)S(1)}, bf16[264,256]{1,0:T(8,128)(2,1)S(1)}, u32[]{:S(2)}, u32[]{:S(2)}) collective-permute-start(bf16[264,256]{1,0:T(8,128)(2,1)S(1)} %get-tuple-element.62), channel_id=1, source_target_pairs={{0,12},{2,14},{4,8},{6,10},{8,4},{10,6},{12,0},{14,2},{16,28},{18,... | collective-permute-start | bytes 405512 | tf_op jit(solution)/shard_map/ppermute | solution.py:342
  39.4 17.9 %collective-permute-start.6 = (bf16[264,256]{1,0:T(8,128)(2,1)S(1)}, bf16[264,256]{1,0:T(8,128)(2,1)S(1)}, u32[]{:S(2)}, u32[]{:S(2)}) collective-permute-start(bf16[264,256]{1,0:T(8,128)(2,1)S(1)} %get-tuple-element.63), channel_id=1, source_target_pairs={{0,14},{2,12},{4,10},{6,8},{8,6},{10,4},{12,2},{14,0},{16,30},{18,... | collective-permute-start | bytes 405512 | tf_op jit(solution)/shard_map/ppermute | solution.py:342
  67.6 31.8 %collective-permute-start.25 = (bf16[8,128,256]{2,1,0:T(8,128)(2,1)S(1)}, bf16[8,128,256]{2,1,0:T(8,128)(2,1)S(1)}, u32[]{:S(2)}, u32[]{:S(2)}) collective-permute-start(bf16[8,128,256]{2,1,0:T(8,128)(2,1)S(1)} %shard_map.159.back.rows.refs_4_), channel_id=1, source_target_pairs={{0,16},{2,18},{4,20},{6,22},{8,24},{10,26},{12,28},{14,30},{16,0},... | collective-permute-start | bytes 1572872 | tf_op jit(solution)/shard_map/ppermute | solution.py:342
  81.8 15.4 %collective-permute-start.21 = (bf16[128,512]{1,0:T(8,128)(2,1)S(1)}, bf16[128,512]{1,0:T(8,128)(2,1)S(1)}, u32[]{:S(2)}, u32[]{:S(2)}) collective-permute-start(bf16[128,512]{1,0:T(8,128)(2,1)S(1)} %shard_map.156.refs_0_), channel_id=1, source_target_pairs={{0,16},{2,18},{4,20},{6,22},{8,24},{10,26},{12,28},{14,30},{16,0},... | collective-permute-start | bytes 393224 | tf_op jit(solution)/shard_map/ppermute | solution.py:342
  83.8 14.3 %collective-permute-start.29 = (bf16[256,256]{1,0:T(8,128)(2,1)S(1)}, bf16[256,256]{1,0:T(8,128)(2,1)S(1)}, u32[]{:S(2)}, u32[]{:S(2)}) collective-permute-start(bf16[256,256]{1,0:T(8,128)(2,1)S(1)} %get-tuple-element.90), channel_id=1, source_target_pairs={{0,8},{2,10},{4,12},{6,14},{8,0},{10,2},{12,4},{14,6},{16,24},{18,... | collective-permute-start | bytes 393224 | tf_op jit(solution)/shard_map/ppermute | solution.py:342
  84.4 16.5 %collective-permute-start.30 = (bf16[256,256]{1,0:T(8,128)(2,1)S(1)}, bf16[256,256]{1,0:T(8,128)(2,1)S(1)}, u32[]{:S(2)}, u32[]{:S(2)}) collective-permute-start(bf16[256,256]{1,0:T(8,128)(2,1)S(1)} %get-tuple-element.91), channel_id=1, source_target_pairs={{0,10},{2,8},{4,14},{6,12},{8,2},{10,0},{12,6},{14,4},{16,26},{18,... | collective-permute-start | bytes 393224 | tf_op jit(solution)/shard_map/ppermute | solution.py:342
  85.9 20.1 %collective-permute-start.31 = (bf16[256,256]{1,0:T(8,128)(2,1)S(1)}, bf16[256,256]{1,0:T(8,128)(2,1)S(1)}, u32[]{:S(2)}, u32[]{:S(2)}) collective-permute-start(bf16[256,256]{1,0:T(8,128)(2,1)S(1)} %get-tuple-element.92), channel_id=1, source_target_pairs={{0,12},{2,14},{4,8},{6,10},{8,4},{10,6},{12,0},{14,2},{16,28},{18,... | collective-permute-start | bytes 393224 | tf_op jit(solution)/shard_map/ppermute | solution.py:342
  97.1 10.3 %collective-permute-start.32 = (bf16[256,256]{1,0:T(8,128)(2,1)S(1)}, bf16[256,256]{1,0:T(8,128)(2,1)S(1)}, u32[]{:S(2)}, u32[]{:S(2)}) collective-permute-start(bf16[256,256]{1,0:T(8,128)(2,1)S(1)} %get-tuple-element.93), channel_id=1, source_target_pairs={{0,14},{2,12},{4,10},{6,8},{8,6},{10,4},{12,2},{14,0},{16,30},{18,... | collective-permute-start | bytes 393224 | tf_op jit(solution)/shard_map/ppermute | solution.py:342
  98.1 11.4 %collective-permute-start.24 = (bf16[128,512]{1,0:T(8,128)(2,1)S(1)}, bf16[128,512]{1,0:T(8,128)(2,1)S(1)}, u32[]{:S(2)}, u32[]{:S(2)}) collective-permute-start(bf16[128,512]{1,0:T(8,128)(2,1)S(1)} %shard_map.157.refs_0_), channel_id=1, source_target_pairs={{0,6},{2,4},{4,2},{6,0},{8,14},{10,12},{12,10},{14,8},{16,22},{18,... | collective-permute-start | bytes 393224 | tf_op jit(solution)/shard_map/ppermute | solution.py:342
  99.4 11.9 %collective-permute-start.23 = (bf16[128,512]{1,0:T(8,128)(2,1)S(1)}, bf16[128,512]{1,0:T(8,128)(2,1)S(1)}, u32[]{:S(2)}, u32[]{:S(2)}) collective-permute-start(bf16[128,512]{1,0:T(8,128)(2,1)S(1)} %shard_map.157.refs_0_), channel_id=1, source_target_pairs={{0,4},{2,6},{4,0},{6,2},{8,12},{10,14},{12,8},{14,10},{16,20},{18,... | collective-permute-start | bytes 393224 | tf_op jit(solution)/shard_map/ppermute | solution.py:342
  100.9 11.5 %collective-permute-start.22 = (bf16[128,512]{1,0:T(8,128)(2,1)S(1)}, bf16[128,512]{1,0:T(8,128)(2,1)S(1)}, u32[]{:S(2)}, u32[]{:S(2)}) collective-permute-start(bf16[128,512]{1,0:T(8,128)(2,1)S(1)} %shard_map.157.refs_0_), channel_id=1, source_target_pairs={{0,2},{2,0},{4,6},{6,4},{8,10},{10,8},{12,14},{14,12},{16,18},{18,... | collective-permute-start | bytes 393224 | tf_op jit(solution)/shard_map/ppermute | solution.py:342
  106.0 8.9 %collective-permute-start.33 = (bf16[256,256]{1,0:T(8,128)(2,1)S(1)}, bf16[256,256]{1,0:T(8,128)(2,1)S(1)}, u32[]{:S(2)}, u32[]{:S(2)}) collective-permute-start(bf16[256,256]{1,0:T(8,128)(2,1)S(1)} %get-tuple-element.95), channel_id=1, source_target_pairs={{0,2},{2,0},{4,6},{6,4},{8,10},{10,8},{12,14},{14,12},{16,18},{18,... | collective-permute-start | bytes 393224 | tf_op jit(solution)/shard_map/ppermute | solution.py:342
  107.5 9.2 %collective-permute-start.34 = (bf16[256,256]{1,0:T(8,128)(2,1)S(1)}, bf16[256,256]{1,0:T(8,128)(2,1)S(1)}, u32[]{:S(2)}, u32[]{:S(2)}) collective-permute-start(bf16[256,256]{1,0:T(8,128)(2,1)S(1)} %get-tuple-element.96), channel_id=1, source_target_pairs={{0,4},{2,6},{4,0},{6,2},{8,12},{10,14},{12,8},{14,10},{16,20},{18,... | collective-permute-start | bytes 393224 | tf_op jit(solution)/shard_map/ppermute | solution.py:342
  109.5 11.1 %collective-permute-start.35 = (bf16[256,256]{1,0:T(8,128)(2,1)S(1)}, bf16[256,256]{1,0:T(8,128)(2,1)S(1)}, u32[]{:S(2)}, u32[]{:S(2)}) collective-permute-start(bf16[256,256]{1,0:T(8,128)(2,1)S(1)} %get-tuple-element.97), channel_id=1, source_target_pairs={{0,6},{2,4},{4,2},{6,0},{8,14},{10,12},{12,10},{14,8},{16,22},{18,... | collective-permute-start | bytes 393224 | tf_op jit(solution)/shard_map/ppermute | solution.py:342
  111.3 9.4 %collective-permute-start.36 = (bf16[256,256]{1,0:T(8,128)(2,1)S(1)}, bf16[256,256]{1,0:T(8,128)(2,1)S(1)}, u32[]{:S(2)}, u32[]{:S(2)}) collective-permute-start(bf16[256,256]{1,0:T(8,128)(2,1)S(1)} %get-tuple-element.98), channel_id=1, source_target_pairs={{0,8},{2,10},{4,12},{6,14},{8,0},{10,2},{12,4},{14,6},{16,24},{18,... | collective-permute-start | bytes 393224 | tf_op jit(solution)/shard_map/ppermute | solution.py:342
  112.4 8.7 %collective-permute-start.37 = (bf16[256,256]{1,0:T(8,128)(2,1)S(1)}, bf16[256,256]{1,0:T(8,128)(2,1)S(1)}, u32[]{:S(2)}, u32[]{:S(2)}) collective-permute-start(bf16[256,256]{1,0:T(8,128)(2,1)S(1)} %get-tuple-element.99), channel_id=1, source_target_pairs={{0,10},{2,8},{4,14},{6,12},{8,2},{10,0},{12,6},{14,4},{16,26},{18,... | collective-permute-start | bytes 393224 | tf_op jit(solution)/shard_map/ppermute | solution.py:342
  114.9 9.1 %collective-permute-start.38 = (bf16[256,256]{1,0:T(8,128)(2,1)S(1)}, bf16[256,256]{1,0:T(8,128)(2,1)S(1)}, u32[]{:S(2)}, u32[]{:S(2)}) collective-permute-start(bf16[256,256]{1,0:T(8,128)(2,1)S(1)} %get-tuple-element.100), channel_id=1, source_target_pairs={{0,12},{2,14},{4,8},{6,10},{8,4},{10,6},{12,0},{14,2},{16,28},{18,... | collective-permute-start | bytes 393224 | tf_op jit(solution)/shard_map/ppermute | solution.py:342
  116.6 9.3 %collective-permute-start.39 = (bf16[256,256]{1,0:T(8,128)(2,1)S(1)}, bf16[256,256]{1,0:T(8,128)(2,1)S(1)}, u32[]{:S(2)}, u32[]{:S(2)}) collective-permute-start(bf16[256,256]{1,0:T(8,128)(2,1)S(1)} %get-tuple-element.101), channel_id=1, source_target_pairs={{0,14},{2,12},{4,10},{6,8},{8,6},{10,4},{12,2},{14,0},{16,30},{18,... | collective-permute-start | bytes 393224 | tf_op jit(solution)/shard_map/ppermute | solution.py:342
  (31 other events, 222.0 us)
